TPU v7x, 256 devices: a whole 4x4x8 slice. The times are simulated.
256 devices in a mesh: seq: 16 (over x_lo, z), mp: 8 (over y, core), dp: 2 (over x_hi).
Axes of the slice: x: 4 (x_hi: 2, x_lo: 2; x = x_hi * 2 + x_lo), y: 4, z: 8, core: 2. Of those that a mesh axis runs over, the one named last changes fastest.
Arguments:
- residual_in: bfloat16 [12288, 2048], P(('dp', 'seq')), parts along dimension 0, may hold values from -6 to 6
- queries: bfloat16 [12288, 2048], P(('dp', 'seq'), 'mp'), parts along dimension 0, may hold values from -30 to 30
- keys: bfloat16 [12288, 2048], P(('dp', 'seq'), 'mp'), parts along dimension 0, may hold values from -10 to 10
- values: bfloat16 [12288, 2048], P(('dp', 'seq'), 'mp'), parts along dimension 0, may hold values from -6 to 6
- w_out: bfloat16 [2048, 2048], P('mp', 'seq'), may hold values from -0.1875 to 0.1875
- conv_value: bfloat16 [2048, 2048], P('seq', 'mp'), may hold values from -0.125 to 0.125
- conv_gate: bfloat16 [2048, 2048], P('seq', 'mp'), may hold values from -0.125 to 0.125
- depth_kernel: float32 [31, 2048], P(None, 'mp'), may hold values from -2 to 2
- conv_out: bfloat16 [2048, 2048], P('mp', 'seq'), may hold values from -0.25 to 0.25
- ffn_in: bfloat16 [2048, 8192], P('seq', 'mp'), may hold values from -0.125 to 0.125
- ffn_down: bfloat16 [8192, 2048], P('mp', 'seq'), may hold values from -0.1875 to 0.1875
- ffn_mask: int32 [96, 64], P(('dp', 'seq'), 'mp'), parts along dimension 0, may hold values 0 or 1
Outputs:
- block_out: float32 [12288, 2048], P(('dp', 'seq', 'mp')), parts along dimension 0
There are 2 independent parts, one for each index of `dp`. A program takes and returns all parts, laid end to end along the dimension named above; an argument that names none is the same for every part. Nothing has to cross between parts.
All inputs are finite; a program needn't handle non-finite values. No bound on the sum of `ffn_mask` on one device may be relied on, other than what follows from the above.
Results may differ from a plain program's by a relative error of at most 0.017.
Values may be sent and summed in bfloat16 or wider, within the bound.
A program may use at most 128 MiB of HBM per device.

v0:
```python
import math

import jax
import jax.numpy as jnp
from jax import lax
from jax.sharding import PartitionSpec as P

HEAD_DIM = 128


norm_epsilon = 1e-05


def padded_2(value, sides, width):
    for axis, dim in sides:
        count, length = (lax.axis_size(axis), value.shape[dim])
        up = [(i, (i + 1) % count) for i in range(count - 1)]
        down = [(j, i) for i, j in up]
        last = lax.slice_in_dim(value, length - width, length, axis=dim)
        leading = lax.slice_in_dim(value, 0, width, axis=dim)
        before = lax.ppermute(last, axis, up)
        after = lax.ppermute(leading, axis, down)
        value = jnp.concatenate([before, value, after], axis=dim)
    return value


def layer_norm(stream):
    row_mean = jnp.mean(stream, axis=-1, keepdims=True)
    centered = stream - row_mean
    spread = jnp.mean(centered * centered, axis=-1, keepdims=True)
    return centered * lax.rsqrt(spread + norm_epsilon)


def accumulate_rows(left, weight_piece):
    return jnp.dot(left, weight_piece, preferred_element_type=jnp.float32)


def add_branch(stream, branch_part, factor):
    return stream + factor * lax.psum(branch_part.astype(jnp.bfloat16), "mp").astype(jnp.float32)


def on_device(
    residual_in,
    queries,
    keys,
    values,
    w_out,
    conv_value,
    conv_gate,
    depth_kernel,
    conv_out,
    ffn_in,
    ffn_down,
    ffn_mask,
):
    row_count = queries.shape[0]
    local_width = queries.shape[1]
    heads_here = local_width // HEAD_DIM
    score_scale = 1.0 / math.sqrt(HEAD_DIM)
    query_heads = queries.reshape(row_count, heads_here, HEAD_DIM)
    pieces = (
        lax.all_gather(keys, "seq", axis=0, tiled=True),
        lax.all_gather(values, "seq", axis=0, tiled=True),
    )
    running_max = jnp.full((row_count, heads_here), -1e30, jnp.float32)
    key_heads = pieces[0].reshape(pieces[0].shape[0], heads_here, HEAD_DIM)
    value_heads = pieces[1].reshape(pieces[1].shape[0], heads_here, HEAD_DIM)
    scores = (
        jnp.einsum("qhd,khd->qhk", query_heads, key_heads, preferred_element_type=jnp.float32)
        * score_scale
    )
    new_max = jnp.maximum(running_max, jnp.max(scores, axis=-1))
    exp_scores = jnp.exp(scores - new_max[..., None])
    running_sum = jnp.sum(exp_scores, axis=-1)
    weighted = jnp.einsum(
        "qhk,khd->qhd",
        exp_scores.astype(jnp.bfloat16),
        value_heads,
        preferred_element_type=jnp.float32,
    )
    weighted, running_max, running_sum = (weighted, new_max, running_sum)
    heads_out = (
        (weighted / running_sum[..., None]).reshape(row_count, local_width).astype(jnp.bfloat16)
    )
    attn_part = jnp.dot(
        heads_out,
        lax.all_gather(w_out, "seq", axis=1, tiled=True),
        preferred_element_type=jnp.float32,
    )
    share_count = row_count // lax.axis_size("mp")
    stream = residual_in.astype(jnp.float32)
    stream = add_branch(stream, attn_part, 1.0)
    norm_one = layer_norm(stream).astype(jnp.bfloat16)
    conv_width = conv_value.shape[1]
    pieces = (
        lax.all_gather(conv_value, "seq", axis=0, tiled=True),
        lax.all_gather(conv_gate, "seq", axis=0, tiled=True),
    )
    value_half = accumulate_rows(norm_one, pieces[0])
    gate_half = accumulate_rows(norm_one, pieces[1])
    gated_units = (value_half * jax.nn.sigmoid(gate_half)).astype(jnp.bfloat16)
    half_width = depth_kernel.shape[0] // 2
    padded = padded_2(gated_units, (("seq", 0),), half_width)
    depth_out = jnp.zeros((row_count, conv_width), jnp.float32)
    for tap_index in range(depth_kernel.shape[0]):
        depth_out = depth_out + depth_kernel[tap_index] * padded[
            tap_index : tap_index + row_count
        ].astype(jnp.float32)
    activated = jax.nn.silu(depth_out).astype(jnp.bfloat16)
    conv_part = jnp.dot(
        activated,
        lax.all_gather(conv_out, "seq", axis=1, tiled=True),
        preferred_element_type=jnp.float32,
    )
    stream = add_branch(stream, conv_part, 1.0)
    norm_two = layer_norm(stream).astype(jnp.bfloat16)
    pre_hidden = accumulate_rows(norm_two, lax.all_gather(ffn_in, "seq", axis=0, tiled=True))
    tile_count, block_count = ffn_mask.shape
    hidden = (
        jax.nn.silu(pre_hidden).reshape(tile_count, row_count // tile_count, block_count, -1)
        * ffn_mask.astype(jnp.float32)[:, None, :, None]
    )
    hidden = hidden.reshape(row_count, -1).astype(jnp.bfloat16)
    ffn_part = jnp.dot(
        hidden,
        lax.all_gather(ffn_down, "seq", axis=1, tiled=True),
        preferred_element_type=jnp.float32,
    )
    stream = add_branch(stream, ffn_part, 0.5)
    stream = lax.dynamic_slice_in_dim(stream, lax.axis_index("mp") * share_count, share_count, 0)
    return layer_norm(stream)


def solution(mesh):
    in_specs = (
        P(("dp", "seq"), None),
        P(("dp", "seq"), "mp"),
        P(("dp", "seq"), "mp"),
        P(("dp", "seq"), "mp"),
        P("mp", "seq"),
        P("seq", "mp"),
        P("seq", "mp"),
        P(None, "mp"),
        P("mp", "seq"),
        P("seq", "mp"),
        P("mp", "seq"),
        P(("dp", "seq"), "mp"),
    )
    out_specs = P(("dp", "seq", "mp"), None)
    return jax.shard_map(
        on_device, mesh=mesh, in_specs=in_specs, out_specs=out_specs, check_vma=False
    )
```

profile of v0, /device:TPU:1, one launch (start us, length us, event | category | flops | bytes accessed | tf_op | source)
XLA Modules:
  0.0 828.9 jit_solution(12674205064811095764)
XLA Ops:
  6.5 1.8 copy.16
  9.9 66.8 %all-gather.9.cloned.1.call-done = bf16[6144,256]{0,1:T(8,128)(2,1)} async-done(((bf16[384,256]{0,1:T(8,128)(2,1)}), bf16[6144,256]{0,1:T(8,128)(2,1)}) %all-gather.9.cloned.1.call-update) | async-done | bytes 3145744 | tf_op jit(solution)/shard_map/all_gather | solution.py:62
  76.6 11.3 %bitcast_reduce_fusion = (f32[384,2]{0,1:T(2,128)S(1)}, f32[2,6144,384]{2,1,0:T(8,128)}) fusion(bf16[6144,2,128]{0,2,1:T(8,128)(2,1)} %bitcast.85, bf16[384,256]{1,0:T(8,128)(2,1)S(1)} %copy-done), kind=kOutput, calls=%fused_computation.1 | convolution fusion | flops 1217395968 | bytes 22219776 | tf_op jit(solution)/shard_map/qhd,khd->qhk/dot_general | solution.py:69
  88.0 61.9 %all-gather.11.cloned.1.call-done = bf16[6144,256]{1,0:T(8,128)(2,1)} async-done(((bf16[384,256]{1,0:T(8,128)(2,1)}), bf16[6144,256]{1,0:T(8,128)(2,1)}) %all-gather.11.cloned.1.call-update) | async-done | bytes 3145744 | tf_op jit(solution)/shard_map/all_gather | solution.py:63
  149.9 4.7 copy.19
  154.6 9.4 %fusion.1 = f32[384,2]{0,1:T(2,128)S(1)} fusion(f32[2,6144,384]{2,1,0:T(8,128)} %get-tuple-element.41, f32[384,2]{0,1:T(2,128)S(1)} %broadcast_maximum_fusion), kind=kLoop, calls=%fused_computation.3 | loop fusion | flops 14155008 | bytes 18880512 | tf_op jit(solution)/shard_map/reduce_sum | solution.py:74
  164.0 10.8 %fusion.22 = bf16[384,2,128]{0,2,1:T(8,128)(2,1)S(1)} fusion(bf16[6144,2,128]{0,2,1:T(8,128)(2,1)} %bitcast.84, f32[2,6144,384]{2,1,0:T(8,128)} %get-tuple-element.41, f32[384,2]{0,1:T(2,128)S(1)} %broadcast_maximum_fusion, f32[384,2]{0,1:T(2,128)S(1)} %fusion.1), kind=kOutput, calls=%fused_computation.59 | convolution fusion | flops 1222311936 | bytes 22222848 | tf_op jit(solution)/shard_map/qhk,khd->qhd/dot_general | solution.py:75
  174.8 37.5 %all-gather.13.cloned.1.call-done = bf16[256,2048]{1,0:T(8,128)(2,1)} async-done(((bf16[256,128]{1,0:T(8,128)(2,1)}), bf16[256,2048]{1,0:T(8,128)(2,1)}) %all-gather.13.cloned.1.call-update) | async-done | bytes 1048592 | tf_op jit(solution)/shard_map/all_gather | solution.py:87
  212.3 3.0 convolution_convert_fusion.2
  216.6 0.7 all-gather.19.cloned.1.call-update
  217.5 75.8 %all-reduce.4.cloned.1.call-done = bf16[384,2048]{1,0:T(8,128)(2,1)} async-done(((bf16[384,2048]{1,0:T(8,128)(2,1)}), bf16[384,2048]{1,0:T(8,128)(2,1)}) %all-reduce.4.cloned.1.call-update) | async-done | bytes 1572880 | tf_op jit(solution)/shard_map/psum | solution.py:39
  293.3 2.0 fusion.7
  295.3 0.7 multiply_reduce_fusion.1
  296.0 1.8 multiply_convert_fusion.1
  297.8 56.6 %all-gather.17.cloned.1.call-done = bf16[2048,256]{1,0:T(8,128)(2,1)} async-done(((bf16[128,256]{1,0:T(8,128)(2,1)}), bf16[2048,256]{1,0:T(8,128)(2,1)}) %all-gather.17.cloned.1.call-update) | async-done | bytes 1048592 | tf_op jit(solution)/shard_map/all_gather | solution.py:97
  354.4 3.0 fusion.14
  357.4 65.0 %all-gather.15.cloned.1.call-done = bf16[2048,256]{1,0:T(8,128)(2,1)} async-done(((bf16[128,256]{1,0:T(8,128)(2,1)}), bf16[2048,256]{1,0:T(8,128)(2,1)}) %all-gather.15.cloned.1.call-update) | async-done | bytes 1048592 | tf_op jit(solution)/shard_map/all_gather | solution.py:96
  422.4 2.4 fusion.18
  424.8 2.3 collective-permute-start
  427.0 1.3 collective-permute-start.1
  428.4 57.8 %all-gather.19.cloned.1.call-done = bf16[256,2048]{1,0:T(8,128)(2,1)} async-done(((bf16[256,128]{1,0:T(8,128)(2,1)}), bf16[256,2048]{1,0:T(8,128)(2,1)}) %all-gather.19.cloned.1.call-update) | async-done | bytes 1048592 | tf_op jit(solution)/shard_map/all_gather | solution.py:112
  486.2 10.9 %convolution_convert_fusion.1 = bf16[384,2048]{1,0:T(8,128)(2,1)} fusion(bf16[256,2048]{1,0:T(8,128)(2,1)} %all-gather.19.cloned.1.call-done, bf16[384,256]{1,0:T(8,128)(2,1)} %copy-done.6, bf16[15,256]{1,0:T(8,128)(2,1)S(1)} %collective-permute-done.1, bf16[15,256]{1,0:T(8,128)(2,1)S(1)} %collective-permute-done, f32[256]{0:T(256)S(1)} %bitcast.117, ...), kind=kOutput, calls=%fused_computation.15 | convolution fusion | flops 421822464 | bytes 2865152 | tf_op jit(solution)/shard_map/dot_general | solution.py:110
  498.5 76.6 %all-reduce.6.cloned.1.call-done = bf16[384,2048]{1,0:T(8,128)(2,1)} async-done(((bf16[384,2048]{1,0:T(8,128)(2,1)}), bf16[384,2048]{1,0:T(8,128)(2,1)}) %all-reduce.6.cloned.1.call-update) | async-done | bytes 1572880 | tf_op jit(solution)/shard_map/psum | solution.py:39
  575.1 2.1 fusion.61
  577.2 1.7 copy-done.3
  579.3 65.5 %all-gather.21.cloned.1.call-done = bf16[2048,1024]{1,0:T(8,128)(2,1)} async-done(((bf16[128,1024]{1,0:T(8,128)(2,1)}), bf16[2048,1024]{1,0:T(8,128)(2,1)}) %all-gather.21.cloned.1.call-update) | async-done | bytes 4194320 | tf_op jit(solution)/shard_map/all_gather | solution.py:117
  644.8 85.4 %all-gather.23.cloned.1.call-done = bf16[1024,2048]{1,0:T(8,128)(2,1)} async-done(((bf16[1024,128]{1,0:T(8,128)(2,1)}), bf16[1024,2048]{1,0:T(8,128)(2,1)}) %all-gather.23.cloned.1.call-update) | async-done | bytes 4194320 | tf_op jit(solution)/shard_map/all_gather | solution.py:126
  730.4 9.5 %convolution_convert_fusion = bf16[384,2048]{1,0:T(8,128)(2,1)} fusion(bf16[1024,2048]{1,0:T(8,128)(2,1)} %all-gather.23.cloned.1.call-done, f32[48,8,8,128]{3,2,1,0:T(8,128)S(1)} %bitcast.86, bf16[2048,1024]{1,0:T(8,128)(2,1)} %all-gather.21.cloned.1.call-done, f32[384,2048]{1,0:T(8,128)} %copy-done.3, f32[384]{0:T(512)S(1)} %add_rsqrt_fusion, ...), kind=kOutput, calls=%fused_computation.14 | convolution fusion | flops 3226730496 | bytes 14683136 | tf_op jit(solution)/shard_map/dot_general | solution.py:124
  739.9 77.9 %all-reduce.8.cloned.1.call-done = bf16[384,2048]{1,0:T(8,128)(2,1)} async-done(((bf16[384,2048]{1,0:T(8,128)(2,1)}), bf16[384,2048]{1,0:T(8,128)(2,1)}) %all-reduce.8.cloned.1.call-update) | async-done | bytes 1572880 | tf_op jit(solution)/shard_map/psum | solution.py:39
  817.8 1.3 fusion.56
  819.1 1.3 multiply_reduce_fusion.2
  820.4 2.0 subtract_multiply_fusion
  (49 shorter events, 5.0 us)
Async XLA Ops:
  6.5 70.1 %copy-start = (bf16[384,256]{1,0:T(8,128)(2,1)S(1)}, bf16[384,256]{1,0:T(8,128)(2,1)}, u32[]{:S(2)}) copy-start(bf16[384,256]{1,0:T(8,128)(2,1)} %param.13) | copy-start | bytes 589828
  6.5 70.1 %all-gather.9.cloned.1.call-start = ((), (), s32[]{:S(2)}) async-start(), calls=%async_computation | async-start | bytes 3342336 | tf_op jit(solution)/shard_map/all_gather | solution.py:62
  8.3 141.5 %all-gather.11.cloned.1.call-start = ((), (), s32[]{:S(2)}) async-start(), calls=%async_computation.1 | async-start | bytes 3342336 | tf_op jit(solution)/shard_map/all_gather | solution.py:63
  9.1 203.2 %all-gather.13.cloned.1.call-start = ((), (), s32[]{:S(2)}) async-start(), calls=%async_computation.2 | async-start | bytes 1114112 | tf_op jit(solution)/shard_map/all_gather | solution.py:87
  9.8 283.5 %all-reduce.4.cloned.1.call-start = ((), (), s32[]{:S(2)}) async-start(), calls=%async_computation.3 | async-start | bytes 3145728 | tf_op jit(solution)/shard_map/psum | solution.py:39
  174.8 42.7 %copy-start.4 = (f32[31,256]{1,0:T(8,128)S(1)}, f32[31,256]{1,0:T(8,128)}, u32[]{:S(2)}) copy-start(f32[31,256]{1,0:T(8,128)} %param.19) | copy-start | bytes 95236
  174.8 118.5 %copy-start.1 = (bf16[384,2048]{1,0:T(8,128)(2,1)S(1)}, bf16[384,2048]{1,0:T(8,128)(2,1)}, u32[]{:S(2)}) copy-start(bf16[384,2048]{1,0:T(8,128)(2,1)} %param.12) | copy-start | bytes 4718596
  215.3 139.1 %all-gather.17.cloned.1.call-start = ((), (), s32[]{:S(2)}) async-start(), calls=%async_computation.5 | async-start | bytes 1114112 | tf_op jit(solution)/shard_map/all_gather | solution.py:97
  215.9 206.5 %all-gather.15.cloned.1.call-start = ((), (), s32[]{:S(2)}) async-start(), calls=%async_computation.4 | async-start | bytes 1114112 | tf_op jit(solution)/shard_map/all_gather | solution.py:96
  216.5 269.7 %all-gather.19.cloned.1.call-start = ((), (), s32[]{:S(2)}) async-start(), calls=%async_computation.6 | async-start | bytes 1114112 | tf_op jit(solution)/shard_map/all_gather | solution.py:112
  217.3 357.8 %all-reduce.6.cloned.1.call-start = ((), (), s32[]{:S(2)}) async-start(), calls=%async_computation.7 | async-start | bytes 3145728 | tf_op jit(solution)/shard_map/psum | solution.py:39
  293.3 2.0 copy-start.2
  424.8 3.6 copy-start.6
  424.8 61.4 %collective-permute-start = (bf16[15,256]{1,0:T(8,128)(2,1)S(1)}, bf16[15,256]{1,0:T(8,128)(2,1)S(1)}, u32[]{:S(2)}, u32[]{:S(2)}) collective-permute-start(bf16[15,256]{1,0:T(8,128)(2,1)S(1)} %get-tuple-element.7), channel_id=1, source_target_pairs={{0,16},{16,32},{32,48},{48,64},{64,80},{80,96},{96,112},{112,128},... | collective-permute-start | bytes 23048 | tf_op jit(solution)/shard_map/ppermute | solution.py:21
  427.0 59.2 %collective-permute-start.1 = (bf16[15,256]{1,0:T(8,128)(2,1)S(1)}, bf16[15,256]{1,0:T(8,128)(2,1)S(1)}, u32[]{:S(2)}, u32[]{:S(2)}) collective-permute-start(bf16[15,256]{1,0:T(8,128)(2,1)S(1)} %get-tuple-element.8), channel_id=1, source_target_pairs={{16,0},{32,16},{48,32},{64,48},{80,64},{96,80},{112,96},{128,112},... | collective-permute-start | bytes 23048 | tf_op jit(solution)/shard_map/ppermute | solution.py:22
  486.2 12.3 %copy-start.5 = (s32[3,8]{1,0:T(4,128)S(1)}, s32[3,8]{1,0:T(4,128)}, u32[]{:S(2)}) copy-start(s32[3,8]{1,0:T(4,128)} %param.23) | copy-start | bytes 292
  497.1 147.7 %all-gather.21.cloned.1.call-start = ((), (), s32[]{:S(2)}) async-start(), calls=%async_computation.8 | async-start | bytes 4456448 | tf_op jit(solution)/shard_map/all_gather | solution.py:117
  497.8 232.4 %all-gather.23.cloned.1.call-start = ((), (), s32[]{:S(2)}) async-start(), calls=%async_computation.9 | async-start | bytes 4456448 | tf_op jit(solution)/shard_map/all_gather | solution.py:126
  498.4 319.4 %all-reduce.8.cloned.1.call-start = ((), (), s32[]{:S(2)}) async-start(), calls=%async_computation.10 | async-start | bytes 3145728 | tf_op jit(solution)/shard_map/psum | solution.py:39
  577.2 1.7 copy-start.3
Sparse Core Ops, SparseCore 0:
  9.1 67.4 all-gather.8
  78.4 71.4 all-gather.10
  151.6 60.6 all-gather.12
  215.5 77.7 all-reduce.3
  294.9 59.4 all-gather.16
  356.0 66.3 all-gather.14
  424.1 62.0 all-gather.18
  497.2 77.7 all-reduce.5
  576.9 67.9 all-gather.20
  646.4 83.8 all-gather.22
  740.0 77.7 all-reduce.7
where the time goes:
time: 830 us; the launch traced here: 829 us
  waiting for transfers between devices  731 us (88%)
  matrix products  50.8 us (6%)
  other arithmetic  21 us (3%)
  between operations  13.4 us (2%)
  local copies, waits for them, and re-layouts  8.4 us (1%)
    psum x3, waiting for transfers between devices, add_branch(): lax.psum(branch_part.astype(jnp.bfloat16), 'mp').astype(jnp.float32)  230 us
    all_gather x1, waiting for transfers between devices, on_device(): lax.all_gather(ffn_down, 'seq', axis=1, tiled=True)  85.4 us
    all_gather x1, waiting for transfers between devices, on_device(): lax.all_gather(keys, 'seq', axis=0, tiled=True)  66.8 us
    all_gather x1, waiting for transfers between devices, on_device(): lax.all_gather(ffn_in, 'seq', axis=0, tiled=True)  65.5 us
    all_gather x1, waiting for transfers between devices, on_device(): lax.all_gather(conv_value, 'seq', axis=0, tiled=True)  65 us
    all_gather x1, waiting for transfers between devices, on_device(): lax.all_gather(values, 'seq', axis=0, tiled=True)  61.9 us
    all_gather x1, waiting for transfers between devices, on_device(): lax.all_gather(conv_out, 'seq', axis=1, tiled=True)  57.8 us
    all_gather x1, waiting for transfers between devices, on_device(): lax.all_gather(conv_gate, 'seq', axis=0, tiled=True)  56.6 us
  transfers between devices with their start and end apart: 13, of which 11 were waited for; matrix products, arithmetic and copies ran while one was open for 6% of the time, Pallas kernels for 0%

commit v1 on v0

v1 whole, which is shorter than its diff:
```python
import math

import jax
import jax.numpy as jnp
from jax import lax
from jax.experimental import pallas as pl
from jax.experimental.pallas import tpu as pltpu
from jax.sharding import PartitionSpec as P

MESH = pl.DeviceIdType.MESH
BF, F32 = jnp.bfloat16, jnp.float32
HD = 128
NZ = 8
NY = 4
TOK = 384
ROWS = 48
D = 2048
EPS = 1e-05
TAPS = 31
BQ = 256
RIGHT, LEFT = 0, 1
HOPS_A, HOPS_B = (4, 3), (3, 4)


def layer_norm(x):
    mean = jnp.mean(x, axis=-1, keepdims=True)
    cen = x - mean
    var = jnp.mean(cen * cen, axis=-1, keepdims=True)
    return cen * lax.rsqrt(var + EPS)


def block_kernel(
    res_hbm, q_hbm, k_hbm, v_hbm, wo_hbm, cval_hbm, cgate_hbm, dk_ref, co_hbm, fi_hbm, fd_hbm, mask_ref,
    out_ref,
    qb, kb, vb, m_s, l_s, acc, ob, ho, wo, cv, co, fi, fd, res, stream, ps, xs, xr, rs, rr, nb,
    gp, sh, gs, gr, act, hid, mrow,
    loc, qx_s, qx_r, kv1_s, kv1_r, kv_s, kv_r, wz_s, wz_r, wx_s, wx_r, o_s, o_r,
    pc_s, pc_r, rx_s, rx_r, ag_s, ag_r, agc_s, agc_r, h_s, h_r,
):
    seq, mp, dp = lax.axis_index("seq"), lax.axis_index("mp"), lax.axis_index("dp")
    lo, z = lax.div(seq, NZ), lax.rem(seq, NZ)
    y, c = lax.div(mp, 2), lax.rem(mp, 2)

    def zmod(a):
        return lax.rem(a + 2 * NZ, NZ)

    def ymod(a):
        return lax.rem(a + 2 * NY, NY)

    def dev(s, m, d):
        return {"seq": s, "mp": m, "dp": d}

    zr = dev(lo * NZ + zmod(z + 1), mp, dp)
    zl = dev(lo * NZ + zmod(z - 1), mp, dp)
    other_seq = (1 - lo) * NZ + z
    xr_dev = dev(other_seq, mp, lax.rem(dp + lo, 2))
    xl_dev = dev(other_seq, mp, lax.rem(dp + 1 - lo, 2))
    pair = dev(other_seq, mp, dp)
    core = dev(seq, 2 * y + 1 - c, dp)
    ys = [dev(seq, 2 * ymod(y + d) + c, dp) for d in (1, 2, 3)]
    after = dev(lax.rem(seq + 1, 2 * NZ), mp, dp)
    before = dev(lax.rem(seq + 2 * NZ - 1, 2 * NZ), mp, dp)

    pending = []

    def send(src, dst, ssem, rsem, to):
        d = pltpu.make_async_remote_copy(
            src_ref=src, dst_ref=dst, send_sem=ssem, recv_sem=rsem, device_id=to, device_id_type=MESH
        )
        d.start()
        pending.append(d)

    def arrived(dst, ssem, rsem, frm):
        pltpu.make_async_remote_copy(
            src_ref=dst, dst_ref=dst, send_sem=ssem, recv_sem=rsem, device_id=frm, device_id_type=MESH
        ).wait_recv()

    def local(src, dst, i):
        d = pltpu.make_async_copy(src, dst, loc.at[i])
        d.start()
        return d

    own_cols, far_cols = pl.ds(pl.multiple_of(lo * HD, HD), HD), pl.ds(pl.multiple_of((1 - lo) * HD, HD), HD)
    own_rows = pl.ds(pl.multiple_of(lo * TOK, TOK), TOK)
    far_rows = pl.ds(pl.multiple_of((1 - lo) * TOK, TOK), TOK)

    def col_slot(ref):
        return lambda j: ref.at[:, pl.ds(pl.multiple_of(j * 128, 128), 128)]

    def row_slot(ref):
        return lambda j: ref.at[pl.ds(pl.multiple_of(j * 128, 128), 128), :]

    slots = [col_slot(wo), row_slot(cv), col_slot(co), row_slot(fi), col_slot(fd)]
    my_rows = pl.ds(pl.multiple_of(seq * 128, 128), 128)
    lk = local(k_hbm.at[:, own_cols], kb.at[z, own_rows, :], 0)
    lv = local(v_hbm.at[:, own_cols], vb.at[z, own_rows, :], 1)
    lq = local(q_hbm.at[:, own_cols], qb.at[own_rows, :], 2)
    own = [
        [local(wo_hbm, slots[0](seq), 3)],
        [local(cval_hbm, cv.at[my_rows, 0:256], 4), local(cgate_hbm, cv.at[my_rows, 256:512], 5)],
        [local(co_hbm, slots[2](seq), 6)],
        [local(fi_hbm, slots[3](seq), 7)],
        [local(fd_hbm, slots[4](seq), 8)],
    ]
    lres = local(res_hbm.at[pl.ds(pl.multiple_of(mp * ROWS, ROWS), ROWS), :], res, 9)

    bar = pltpu.get_barrier_semaphore()
    peers = [zr, zl, xr_dev, xl_dev, core, *ys, after, before]
    for p in peers:
        pl.semaphore_signal(bar, inc=1, device_id=p, device_id_type=MESH)
    pl.semaphore_wait(bar, len(peers))

    hbm_of, buf_of, hops_of = (k_hbm, v_hbm), (kb, vb), (HOPS_A, HOPS_B)
    for i, (src, dst) in enumerate(
        ((k_hbm, kb.at[z, own_rows, :]), (v_hbm, vb.at[z, own_rows, :]), (q_hbm, qb.at[own_rows, :]))
    ):
        send(src.at[:, far_cols], dst, qx_s.at[i], qx_r.at[i], pair)
    for a in (0, 1):
        for w, to in ((RIGHT, zr), (LEFT, zl)):
            send(hbm_of[a].at[:, own_cols], buf_of[a].at[z, own_rows, :], kv1_s.at[a, w, 0], kv1_r.at[a, w, 0], to)
    for a in (0, 1):
        half = buf_of[a].at[z, far_rows, :]
        arrived(half, qx_s.at[a], qx_r.at[a], pair)
        for w, to in ((RIGHT, zr), (LEFT, zl)):
            send(half, half, kv1_s.at[a, w, 1], kv1_r.at[a, w, 1], to)

    def kv_relay(s):
        for a in (0, 1):
            for w, frm, to, sign in ((RIGHT, zl, zr, -1), (LEFT, zr, zl, 1)):
                if s > hops_of[a][w]:
                    continue
                slot = zmod(z + sign * s)
                if s == 1:
                    for half, rows in ((0, own_rows), (1, far_rows)):
                        arrived(buf_of[a].at[slot, rows, :], kv1_s.at[a, w, half], kv1_r.at[a, w, half], frm)
                else:
                    arrived(buf_of[a].at[slot], kv_s.at[a, w, s - 2], kv_r.at[a, w, s - 2], frm)
                if s + 1 <= hops_of[a][w]:
                    ref = buf_of[a].at[slot]
                    send(ref, ref, kv_s.at[a, w, s - 1], kv_r.at[a, w, s - 1], to)

    hops_w = [HOPS_A, HOPS_B, HOPS_B, HOPS_A, HOPS_B]

    def x_way(p, k):
        return RIGHT if (p + k) % 2 == 0 else LEFT

    def x_send(p, k, shard):
        w = x_way(p, k)
        ref = slots[p](lo * NZ + shard)
        send(ref, ref, wx_s.at[p, k], wx_r.at[p, k], xr_dev if w == RIGHT else xl_dev)

    def begin(p):
        for d in own[p]:
            d.wait()
        ref = slots[p](seq)
        for w, to in ((RIGHT, zr), (LEFT, zl)):
            send(ref, ref, wz_s.at[p, w, 0], wz_r.at[p, w, 0], to)
        x_send(p, 0, z)

    def relay(p, s):
        for w, frm, to, sign in ((RIGHT, zl, zr, -1), (LEFT, zr, zl, 1)):
            if s > hops_w[p][w]:
                continue
            shard = zmod(z + sign * s)
            ref = slots[p](lo * NZ + shard)
            arrived(ref, wz_s.at[p, w, s - 1], wz_r.at[p, w, s - 1], frm)
            if s + 1 <= hops_w[p][w]:
                send(ref, ref, wz_s.at[p, w, s], wz_r.at[p, w, s], to)
            x_send(p, 7 if s == 4 else 2 * s - 1 + w, shard)

    def weights_done(p):
        for k in range(8):
            shard = z if k == 0 else z + 4 if k == 7 else z - (k + 1) // 2 if k % 2 else z + k // 2
            frm = xl_dev if x_way(p, k) == RIGHT else xr_dev
            arrived(slots[p]((1 - lo) * NZ + zmod(shard)), wx_s.at[p, k], wx_r.at[p, k], frm)

    todo = [
        (1, 1), (1, 2), (3, 0), (2, 1), (1, 3), (2, 2), (1, 4), (2, 3), (3, 1), (2, 4), (4, 0), (3, 2),
        (4, 1), (3, 3), (4, 2), (3, 4), (4, 3), (4, 4),
    ]

    def pump(n):
        for _ in range(min(n, len(todo))):
            p, s = todo.pop(0)
            if s == 0:
                begin(p)
            else:
                relay(p, s)

    def need(p):
        while any(q == p for q, _ in todo):
            pump(1)
        weights_done(p)

    scale2 = math.log2(math.e) / math.sqrt(HD)

    def attend(slot, first=False):
        def body(i, carry):
            rows = pl.ds(pl.multiple_of(i * BQ, BQ), BQ)
            s = lax.dot_general(
                qb[rows, :], kb[slot], (((1,), (1,)), ((), ())), preferred_element_type=F32
            )
            top = jnp.max(s, axis=1, keepdims=True)
            if not first:
                old = m_s[rows, :]
                top = jnp.maximum(top, old[:, :1])
            p = jnp.exp2((s - top) * scale2)
            part = p[:, 0:128]
            for t in range(1, 6):
                part = part + p[:, t * 128 : (t + 1) * 128]
            out = jnp.dot(p.astype(BF), vb[slot], preferred_element_type=F32)
            if not first:
                shrink = jnp.exp2((old - top) * scale2)
                part = part + l_s[rows, :] * shrink
                out = out + acc[rows, :] * shrink
            m_s[rows, :] = jnp.broadcast_to(top, (BQ, 128))
            l_s[rows, :] = part
            acc[rows, :] = out
            return carry

        lax.fori_loop(0, 2 * TOK // BQ, body, 0)

    begin(0)
    arrived(qb.at[far_rows, :], qx_s.at[2], qx_r.at[2], pair)
    lq.wait()
    lk.wait()
    lv.wait()
    attend(z, first=True)
    for s in (1, 2, 3):
        kv_relay(s)
        relay(0, s)
        if s == 2:
            begin(1)
        if s == 3:
            begin(2)
        attend(zmod(z - s))
        attend(zmod(z + s))
    kv_relay(4)
    relay(0, 4)
    attend(zmod(z + 4))

    def finish(rows, blocks):
        o = acc[rows, :] / jnp.sum(l_s[rows, :], axis=1, keepdims=True)
        ob[blocks] = o.astype(BF).reshape(8, ROWS, HD)

    far_blocks, own_blocks = pl.ds((1 - lo) * 8, 8), pl.ds(lo * 8, 8)
    finish(far_rows, far_blocks)
    send(ob.at[far_blocks], ho.at[:, :, own_cols], o_s, o_r, pair)
    finish(own_rows, own_blocks)
    lo_copy = local(ob.at[own_blocks], ho.at[:, :, own_cols], 10)
    for i in range(3):
        for u in range(8):
            mrow[i : i + 1, u * 128 : (u + 1) * 128] = jnp.full((1, 128), mask_ref[i, u].astype(F32))
    lres.wait()
    stream[...] = res[...].astype(F32)
    lo_copy.wait()
    pump(1)
    arrived(ho.at[:, :, far_cols], o_s, o_r, pair)

    def branch(n, left, weight, factor, pumps):
        for mine in (False, True):
            side = c if mine else 1 - c
            lhs = jnp.concatenate([left[2 * b + side] for b in range(NY)], axis=0)
            for j in range(4):
                cols = slice(j * 512, (j + 1) * 512)
                prod = jnp.dot(lhs, weight[:, cols], preferred_element_type=F32).reshape(NY, ROWS, 512)
                if mine:
                    ps[:, :, cols] = prod
                else:
                    xs[n, :, :, cols] = prod.astype(BF)
            if not mine:
                send(xs.at[n], xr.at[n], pc_s.at[n], pc_r.at[n], core)
        pump(pumps[0])
        arrived(xr.at[n], pc_s.at[n], pc_r.at[n], core)
        for d in (2, 1, 3):
            b = ymod(y + d)
            rs[n, d - 1] = (ps[b] + xr[n, b].astype(F32)).astype(BF)
            send(rs.at[n, d - 1], rr.at[n, d - 1], rx_s.at[n, d - 1], rx_r.at[n, d - 1], ys[d - 1])
        total = ps[y] + xr[n, y].astype(F32)
        pump(pumps[1])
        for d in (1, 3, 2):
            arrived(rr.at[n, d - 1], rx_s.at[n, d - 1], rx_r.at[n, d - 1], ys[3 - d])
            total = total + rr[n, d - 1].astype(F32)
        new = stream[...] + factor * total
        stream[...] = new
        return layer_norm(new)

    def share(n, rows, pumps):
        nb[n, mp] = rows.astype(BF)
        mine = nb.at[n, mp]
        for d in (2, 1, 3):
            send(mine, mine, ag_s.at[n, d - 1], ag_r.at[n, d - 1], ys[d - 1])
        send(mine, mine, agc_s.at[n, 0], agc_r.at[n, 0], core)
        pump(pumps)
        for d in (1, 3, 2):
            got = nb.at[n, 2 * ymod(y - d) + c]
            arrived(got, ag_s.at[n, d - 1], ag_r.at[n, d - 1], ys[3 - d])
            send(got, got, agc_s.at[n, d], agc_r.at[n, d], core)
        for d in (0, 1, 3, 2):
            arrived(nb.at[n, 2 * ymod(y - d) + 1 - c], agc_s.at[n, d], agc_r.at[n, d], core)

    need(0)
    norm_one = branch(0, ho, wo, 1.0, (2, 3))
    share(0, norm_one, 3)

    need(1)
    lhs = nb[0].reshape(TOK, D)
    value = jnp.dot(lhs, cv[:, 0:256], preferred_element_type=F32)
    gate = jnp.dot(lhs, cv[:, 256:512], preferred_element_type=F32)
    gated = (value * jax.nn.sigmoid(gate)).astype(BF)
    gs[0] = gated[TOK - 16 :, :]
    gs[1] = gated[:16, :]
    send(gs.at[0], gr.at[0], h_s.at[0], h_r.at[0], after)
    send(gs.at[1], gr.at[1], h_s.at[1], h_r.at[1], before)
    gp[16 : 16 + TOK, :] = gated.astype(F32)
    arrived(gr.at[0], h_s.at[0], h_r.at[0], before)
    arrived(gr.at[1], h_s.at[1], h_r.at[1], after)
    gp[0:16, :] = jnp.where(seq > 0, gr[0].astype(F32), 0.0)
    gp[16 + TOK :, :] = jnp.where(seq < 2 * NZ - 1, gr[1].astype(F32), 0.0)
    for r in range(8):
        sh[r] = gp[r + 1 : r + 1 + TOK + 24, :]

    def depth(i, carry):
        total = jnp.zeros((96, 256), F32)
        for t in range(TAPS):
            total = total + dk_ref[t : t + 1, :] * sh[t % 8, pl.ds(pl.multiple_of(i * 96 + t // 8 * 8, 8), 96), :]
        act[pl.ds(2 * i, 2)] = (total * jax.nn.sigmoid(total)).astype(BF).reshape(2, ROWS, 256)
        return carry

    lax.fori_loop(0, 4, depth, 0)
    need(2)
    norm_two = branch(1, act, co, 1.0, (1, 2))
    share(1, norm_two, 2)

    need(3)

    def ffn(j, carry):
        cols = pl.ds(pl.multiple_of(j * 256, 256), 256)
        pre = jnp.dot(nb[1].reshape(TOK, D), fi[:, cols], preferred_element_type=F32)
        h = (pre * jax.nn.sigmoid(pre)).reshape(3, 128, 256) * mrow[:, cols][:, None, :]
        hid[:, :, cols] = h.astype(BF).reshape(8, ROWS, 256)
        return carry

    lax.fori_loop(0, 4, ffn, 0)
    need(4)
    out_ref[...] = branch(2, hid, fd, 0.5, (0, 0))
    for d in pending:
        d.wait_send()


def on_device(*args):
    dma = pltpu.SemaphoreType.DMA
    any_spec = pl.BlockSpec(memory_space=pl.ANY)
    vmem, smem = pl.BlockSpec(memory_space=pltpu.VMEM), pl.BlockSpec(memory_space=pltpu.SMEM)
    v = pltpu.VMEM
    return pl.pallas_call(
        block_kernel,
        out_shape=jax.ShapeDtypeStruct((ROWS, D), F32),
        in_specs=[any_spec] * 7 + [vmem] + [any_spec] * 3 + [smem],
        out_specs=vmem,
        scratch_shapes=[
            v((2 * TOK, HD), BF), v((NZ, 2 * TOK, HD), BF), v((NZ, 2 * TOK, HD), BF),
            v((2 * TOK, 128), F32), v((2 * TOK, 128), F32), v((2 * TOK, HD), F32),
            v((16, ROWS, HD), BF), v((8, ROWS, 256), BF),
            v((256, D), BF), v((D, 512), BF), v((256, D), BF), v((D, 1024), BF), v((1024, D), BF),
            v((ROWS, D), BF), v((ROWS, D), F32), v((NY, ROWS, D), F32),
            v((3, NY, ROWS, D), BF), v((3, NY, ROWS, D), BF), v((3, 3, ROWS, D), BF), v((3, 3, ROWS, D), BF),
            v((2, 8, ROWS, D), BF),
            v((TOK + 32, 256), F32), v((8, TOK + 24, 256), F32), v((2, 16, 256), BF), v((2, 16, 256), BF),
            v((8, ROWS, 256), BF), v((8, ROWS, 1024), BF), v((3, 1024), F32),
            dma((11,)), dma((3,)), dma((3,)), dma((2, 2, 2)), dma((2, 2, 2)), dma((2, 2, 3)), dma((2, 2, 3)),
            dma((5, 2, 4)), dma((5, 2, 4)), dma((5, 8)), dma((5, 8)), dma(()), dma(()),
            dma((3,)), dma((3,)), dma((3, 3)), dma((3, 3)), dma((2, 3)), dma((2, 3)), dma((2, 4)), dma((2, 4)),
            dma((2,)), dma((2,)),
        ],
        compiler_params=pltpu.CompilerParams(
            collective_id=0, has_side_effects=True, vmem_limit_bytes=60 * 1024 * 1024
        ),
        name="block",
    )(*args)


def solution(mesh):
    in_specs = (
        P(("dp", "seq"), None),
        P(("dp", "seq"), "mp"),
        P(("dp", "seq"), "mp"),
        P(("dp", "seq"), "mp"),
        P("mp", "seq"),
        P("seq", "mp"),
        P("seq", "mp"),
        P(None, "mp"),
        P("mp", "seq"),
        P("seq", "mp"),
        P("mp", "seq"),
        P(("dp", "seq"), "mp"),
    )
    out_specs = P(("dp", "seq", "mp"), None)
    return jax.shard_map(on_device, mesh=mesh, in_specs=in_specs, out_specs=out_specs, check_vma=False)
```

time: 830 us -> 161 us (0.19)
  waiting for transfers between devices: 731 us -> 0 us
  Pallas kernels: 0 us -> 159 us
  matrix products: 50.8 us -> 0 us
  other arithmetic: 21 us -> 0 us
  between operations: 13.4 us -> 0.01 us
    all_gather x8 -> x0, waiting for transfers between devices: 496 us -> none  [the longest x1 85.4 us: on_device(): lax.all_gather(ffn_down, 'seq', axis=1, tiled=True)]
    psum x3 -> x0, waiting for transfers between devices: 230 us -> none  [add_branch(): lax.psum(branch_part.astype(jnp.bfloat16), 'mp').astype(jnp.float32)]
    pallas_call x0 -> x1, Pallas kernels: none -> 159 us  [on_device(): pl.pallas_call(block_kernel, out_shape=jax.ShapeDtypeStruct((ROWS, D), F3...]
    dot_general x7 -> x0, matrix products: 50.8 us -> none  [the longest x1 11.3 us: on_device(): jnp.einsum('qhd,khd->qhk', query_heads, key_heads, preferred_element_type...]
    reduce_sum x7 -> x0, other arithmetic: 17.3 us -> none  [the longest x1 9.43 us: on_device(): running_sum = jnp.sum(exp_scores, axis=-1)]
  transfers between devices with their start and end apart: 13 -> 0, of which waited for: 11 -> 0; matrix products, arithmetic and copies ran while one was open for 6% -> 0% of each run, Pallas kernels for 0% -> 0%
where the time goes in v1:
time: 161 us
  Pallas kernels  159 us (99%)
  local copies, waits for them, and re-layouts  1.77 us (1%)
    pallas_call x1, Pallas kernels, on_device(): pl.pallas_call(block_kernel, out_shape=jax.ShapeDtypeStruct((ROWS, D), F3...  159 us

profile of v1, /device:TPU:1, one launch (start us, length us, event | category | flops | bytes accessed | tf_op | source)
XLA Modules:
  0.0 160.7 jit_solution(15453045783219589307)
XLA Ops:
  0.0 159.0 %block.1 = f32[48,2048]{1,0:T(8,128)} custom-call(bf16[384,2048]{1,0:T(8,128)(2,1)} %res_hbm.1, bf16[384,256]{1,0:T(8,128)(2,1)} %q_hbm.1, bf16[384,256]{1,0:T(8,128)(2,1)} %k_hbm.1, bf16[384,256]{1,0:T(8,128)(2,1)} %v_hbm.1, bf16[256,128]{1,0:T(8,128)(2,1)} %wo_hbm.1, bf16[128,256]{1,0:T(8,128)(2,1)} %cval_hbm.1, bf16[128,256]{1,0:T(8,128)(2,1)} %cgate_hbm.1, ...), custom_call_target="tpu_custom_call" | custom-call | tf_op jit(solution)/shard_map/block/pallas_call | solution.py:356
  159.0 1.8 %copy.14 = f32[48,2048]{1,0:T(8,128)} copy(f32[48,2048]{1,0:T(8,128)} %block.1) | data formatting | bytes 786432

commit v2 on v1

--- a/solution.py
+++ b/solution.py
@@ -20,6 +20,12 @@
 BQ = 256
 RIGHT, LEFT = 0, 1
 HOPS_A, HOPS_B = (4, 3), (3, 4)
+CHUNKS = ROWS // 16
+RELAYS = [
+    (3, 0), (1, 1), (2, 1), (3, 1), (4, 0), (1, 2), (2, 2), (3, 2), (4, 1), (1, 3), (2, 3), (3, 3), (4, 2), (1, 4),
+    (2, 4), (5, 0), (3, 4), (4, 3), (6, 0), (5, 1), (4, 4), (6, 1), (5, 2), (6, 2), (5, 3), (6, 3), (5, 4), (6, 4),
+]
+PUMPS = [3] + [1, 1, 1, 1, 1, 1, 1, 1] + [1, 1] + [1, 1, 1, 1, 1, 1, 1, 1] + [0, 0, 0, 0]
 
 
 def layer_norm(x):
@@ -90,7 +96,10 @@
     def row_slot(ref):
         return lambda j: ref.at[pl.ds(pl.multiple_of(j * 128, 128), 128), :]
 
-    slots = [col_slot(wo), row_slot(cv), col_slot(co), row_slot(fi), col_slot(fd)]
+    slots = [
+        col_slot(wo), row_slot(cv), col_slot(co), row_slot(fi.at[:, 0:512]), row_slot(fi.at[:, 512:1024]),
+        col_slot(fd.at[0:512, :]), col_slot(fd.at[512:1024, :]),
+    ]
     my_rows = pl.ds(pl.multiple_of(seq * 128, 128), 128)
     lk = local(k_hbm.at[:, own_cols], kb.at[z, own_rows, :], 0)
     lv = local(v_hbm.at[:, own_cols], vb.at[z, own_rows, :], 1)
@@ -99,10 +108,12 @@
         [local(wo_hbm, slots[0](seq), 3)],
         [local(cval_hbm, cv.at[my_rows, 0:256], 4), local(cgate_hbm, cv.at[my_rows, 256:512], 5)],
         [local(co_hbm, slots[2](seq), 6)],
-        [local(fi_hbm, slots[3](seq), 7)],
-        [local(fd_hbm, slots[4](seq), 8)],
+        [local(fi_hbm.at[:, 0:512], slots[3](seq), 7)],
+        [local(fi_hbm.at[:, 512:1024], slots[4](seq), 8)],
+        [local(fd_hbm.at[0:512, :], slots[5](seq), 9)],
+        [local(fd_hbm.at[512:1024, :], slots[6](seq), 10)],
     ]
-    lres = local(res_hbm.at[pl.ds(pl.multiple_of(mp * ROWS, ROWS), ROWS), :], res, 9)
+    lres = local(res_hbm.at[pl.ds(pl.multiple_of(mp * ROWS, ROWS), ROWS), :], res, 11)
 
     bar = pltpu.get_barrier_semaphore()
     peers = [zr, zl, xr_dev, xl_dev, core, *ys, after, before]
@@ -118,28 +129,28 @@
     for a in (0, 1):
         for w, to in ((RIGHT, zr), (LEFT, zl)):
             send(hbm_of[a].at[:, own_cols], buf_of[a].at[z, own_rows, :], kv1_s.at[a, w, 0], kv1_r.at[a, w, 0], to)
-    for a in (0, 1):
+
+    def pass_half(a):
         half = buf_of[a].at[z, far_rows, :]
         arrived(half, qx_s.at[a], qx_r.at[a], pair)
         for w, to in ((RIGHT, zr), (LEFT, zl)):
             send(half, half, kv1_s.at[a, w, 1], kv1_r.at[a, w, 1], to)
 
-    def kv_relay(s):
-        for a in (0, 1):
-            for w, frm, to, sign in ((RIGHT, zl, zr, -1), (LEFT, zr, zl, 1)):
-                if s > hops_of[a][w]:
-                    continue
-                slot = zmod(z + sign * s)
-                if s == 1:
-                    for half, rows in ((0, own_rows), (1, far_rows)):
-                        arrived(buf_of[a].at[slot, rows, :], kv1_s.at[a, w, half], kv1_r.at[a, w, half], frm)
-                else:
-                    arrived(buf_of[a].at[slot], kv_s.at[a, w, s - 2], kv_r.at[a, w, s - 2], frm)
-                if s + 1 <= hops_of[a][w]:
-                    ref = buf_of[a].at[slot]
-                    send(ref, ref, kv_s.at[a, w, s - 1], kv_r.at[a, w, s - 1], to)
-
-    hops_w = [HOPS_A, HOPS_B, HOPS_B, HOPS_A, HOPS_B]
+    def kv_relay(a, s):
+        for w, frm, to, sign in ((RIGHT, zl, zr, -1), (LEFT, zr, zl, 1)):
+            if s > hops_of[a][w]:
+                continue
+            slot = zmod(z + sign * s)
+            if s == 1:
+                for half, rows in ((0, own_rows), (1, far_rows)):
+                    arrived(buf_of[a].at[slot, rows, :], kv1_s.at[a, w, half], kv1_r.at[a, w, half], frm)
+            else:
+                arrived(buf_of[a].at[slot], kv_s.at[a, w, s - 2], kv_r.at[a, w, s - 2], frm)
+            if s + 1 <= hops_of[a][w]:
+                ref = buf_of[a].at[slot]
+                send(ref, ref, kv_s.at[a, w, s - 1], kv_r.at[a, w, s - 1], to)
+
+    hops_w = [HOPS_A, HOPS_B, HOPS_A, HOPS_A, HOPS_B, HOPS_A, HOPS_B]
 
     def x_way(p, k):
         return RIGHT if (p + k) % 2 == 0 else LEFT
@@ -150,12 +161,9 @@
         send(ref, ref, wx_s.at[p, k], wx_r.at[p, k], xr_dev if w == RIGHT else xl_dev)
 
     def begin(p):
-        for d in own[p]:
-            d.wait()
         ref = slots[p](seq)
         for w, to in ((RIGHT, zr), (LEFT, zl)):
             send(ref, ref, wz_s.at[p, w, 0], wz_r.at[p, w, 0], to)
-        x_send(p, 0, z)
 
     def relay(p, s):
         for w, frm, to, sign in ((RIGHT, zl, zr, -1), (LEFT, zr, zl, 1)):
@@ -174,13 +182,11 @@
             frm = xl_dev if x_way(p, k) == RIGHT else xr_dev
             arrived(slots[p]((1 - lo) * NZ + zmod(shard)), wx_s.at[p, k], wx_r.at[p, k], frm)
 
-    todo = [
-        (1, 1), (1, 2), (3, 0), (2, 1), (1, 3), (2, 2), (1, 4), (2, 3), (3, 1), (2, 4), (4, 0), (3, 2),
-        (4, 1), (3, 3), (4, 2), (3, 4), (4, 3), (4, 4),
-    ]
-
-    def pump(n):
-        for _ in range(min(n, len(todo))):
+    todo = list(RELAYS)
+    counts = list(PUMPS)
+
+    def pump(n=None):
+        for _ in range(min(counts.pop(0) if n is None else n, len(todo))):
             p, s = todo.pop(0)
             if s == 0:
                 begin(p)
@@ -220,25 +226,30 @@
 
         lax.fori_loop(0, 2 * TOK // BQ, body, 0)
 
+    for d in own[0]:
+        d.wait()
     begin(0)
-    arrived(qb.at[far_rows, :], qx_s.at[2], qx_r.at[2], pair)
+    pass_half(0)
+    pass_half(1)
+    for p in range(len(slots)):
+        if p:
+            for d in own[p]:
+                d.wait()
+        x_send(p, 0, z)
     lq.wait()
     lk.wait()
     lv.wait()
+    arrived(qb.at[far_rows, :], qx_s.at[2], qx_r.at[2], pair)
     attend(z, first=True)
-    for s in (1, 2, 3):
-        kv_relay(s)
+    for s in (1, 2, 3, 4):
+        kv_relay(0, s)
+        if s > 1:
+            attend(zmod(z + s - 1))
+        kv_relay(1, s)
         relay(0, s)
-        if s == 2:
-            begin(1)
-        if s == 3:
-            begin(2)
+        if s in (2, 3):
+            begin(s - 1)
         attend(zmod(z - s))
-        attend(zmod(z + s))
-    kv_relay(4)
-    relay(0, 4)
-    attend(zmod(z + 4))
-
     def finish(rows, blocks):
         o = acc[rows, :] / jnp.sum(l_s[rows, :], axis=1, keepdims=True)
         ob[blocks] = o.astype(BF).reshape(8, ROWS, HD)
@@ -247,72 +258,88 @@
     finish(far_rows, far_blocks)
     send(ob.at[far_blocks], ho.at[:, :, own_cols], o_s, o_r, pair)
     finish(own_rows, own_blocks)
-    lo_copy = local(ob.at[own_blocks], ho.at[:, :, own_cols], 10)
+    lo_copy = local(ob.at[own_blocks], ho.at[:, :, own_cols], 12)
     for i in range(3):
         for u in range(8):
             mrow[i : i + 1, u * 128 : (u + 1) * 128] = jnp.full((1, 128), mask_ref[i, u].astype(F32))
     lres.wait()
     stream[...] = res[...].astype(F32)
     lo_copy.wait()
-    pump(1)
+    pump()
     arrived(ho.at[:, :, far_cols], o_s, o_r, pair)
 
-    def branch(n, left, weight, factor, pumps):
+    def branch(n, left, weight, factor):
         for mine in (False, True):
             side = c if mine else 1 - c
             lhs = jnp.concatenate([left[2 * b + side] for b in range(NY)], axis=0)
             for j in range(4):
                 cols = slice(j * 512, (j + 1) * 512)
                 prod = jnp.dot(lhs, weight[:, cols], preferred_element_type=F32).reshape(NY, ROWS, 512)
-                if mine:
-                    ps[:, :, cols] = prod
-                else:
-                    xs[n, :, :, cols] = prod.astype(BF)
+                for r in range(CHUNKS):
+                    chunk = prod[:, r * 16 : (r + 1) * 16]
+                    if mine:
+                        ps[r, :, :, cols] = chunk
+                    else:
+                        xs[n, r, :, :, cols] = chunk.astype(BF)
             if not mine:
-                send(xs.at[n], xr.at[n], pc_s.at[n], pc_r.at[n], core)
-        pump(pumps[0])
-        arrived(xr.at[n], pc_s.at[n], pc_r.at[n], core)
-        for d in (2, 1, 3):
-            b = ymod(y + d)
-            rs[n, d - 1] = (ps[b] + xr[n, b].astype(F32)).astype(BF)
-            send(rs.at[n, d - 1], rr.at[n, d - 1], rx_s.at[n, d - 1], rx_r.at[n, d - 1], ys[d - 1])
-        total = ps[y] + xr[n, y].astype(F32)
-        pump(pumps[1])
-        for d in (1, 3, 2):
-            arrived(rr.at[n, d - 1], rx_s.at[n, d - 1], rx_r.at[n, d - 1], ys[3 - d])
-            total = total + rr[n, d - 1].astype(F32)
-        new = stream[...] + factor * total
-        stream[...] = new
-        return layer_norm(new)
-
-    def share(n, rows, pumps):
-        nb[n, mp] = rows.astype(BF)
-        mine = nb.at[n, mp]
-        for d in (2, 1, 3):
-            send(mine, mine, ag_s.at[n, d - 1], ag_r.at[n, d - 1], ys[d - 1])
-        send(mine, mine, agc_s.at[n, 0], agc_r.at[n, 0], core)
-        pump(pumps)
-        for d in (1, 3, 2):
-            got = nb.at[n, 2 * ymod(y - d) + c]
-            arrived(got, ag_s.at[n, d - 1], ag_r.at[n, d - 1], ys[3 - d])
-            send(got, got, agc_s.at[n, d], agc_r.at[n, d], core)
-        for d in (0, 1, 3, 2):
-            arrived(nb.at[n, 2 * ymod(y - d) + 1 - c], agc_s.at[n, d], agc_r.at[n, d], core)
+                for r in range(CHUNKS):
+                    send(xs.at[n, r], xr.at[n, r], pc_s.at[n, r], pc_r.at[n, r], core)
+                pump()
+        for r in range(CHUNKS):
+            arrived(xr.at[n, r], pc_s.at[n, r], pc_r.at[n, r], core)
+            for d in (2, 1, 3):
+                b = ymod(y + d)
+                rs[n, r, d - 1] = (ps[r, b] + xr[n, r, b].astype(F32)).astype(BF)
+                send(rs.at[n, r, d - 1], rr.at[n, r, d - 1], rx_s.at[n, r, d - 1], rx_r.at[n, r, d - 1], ys[d - 1])
+        for r in range(CHUNKS):
+            pump()
+            rows = slice(r * 16, (r + 1) * 16)
+            total = ps[r, y] + xr[n, r, y].astype(F32)
+            for d in (1, 3, 2):
+                arrived(rr.at[n, r, d - 1], rx_s.at[n, r, d - 1], rx_r.at[n, r, d - 1], ys[3 - d])
+                total = total + rr[n, r, d - 1].astype(F32)
+            new = stream[rows, :] + factor * total
+            if n == 2:
+                out_ref[rows, :] = layer_norm(new)
+                continue
+            stream[rows, :] = new
+            mine = nb.at[n, mp, rows]
+            nb[n, mp, rows] = layer_norm(new).astype(BF)
+            for d in (2, 1, 3):
+                send(mine, mine, ag_s.at[n, r, d - 1], ag_r.at[n, r, d - 1], ys[d - 1])
+            send(mine, mine, agc_s.at[n, r, 0], agc_r.at[n, r, 0], core)
+        if n == 2:
+            return
+        for r in range(CHUNKS):
+            pump()
+            rows = slice(r * 16, (r + 1) * 16)
+            for d in (1, 3, 2):
+                got = nb.at[n, 2 * ymod(y - d) + c, rows]
+                arrived(got, ag_s.at[n, r, d - 1], ag_r.at[n, r, d - 1], ys[3 - d])
+                send(got, got, agc_s.at[n, r, d], agc_r.at[n, r, d], core)
+        pump()
+        for r in range(CHUNKS):
+            rows = slice(r * 16, (r + 1) * 16)
+            for d in (0, 1, 3, 2):
+                arrived(nb.at[n, 2 * ymod(y - d) + 1 - c, rows], agc_s.at[n, r, d], agc_r.at[n, r, d], core)
 
     need(0)
-    norm_one = branch(0, ho, wo, 1.0, (2, 3))
-    share(0, norm_one, 3)
+    branch(0, ho, wo, 1.0)
 
     need(1)
-    lhs = nb[0].reshape(TOK, D)
-    value = jnp.dot(lhs, cv[:, 0:256], preferred_element_type=F32)
-    gate = jnp.dot(lhs, cv[:, 256:512], preferred_element_type=F32)
-    gated = (value * jax.nn.sigmoid(gate)).astype(BF)
-    gs[0] = gated[TOK - 16 :, :]
-    gs[1] = gated[:16, :]
+
+    def glu(rows):
+        value = jnp.dot(rows, cv[:, 0:256], preferred_element_type=F32)
+        gate = jnp.dot(rows, cv[:, 256:512], preferred_element_type=F32)
+        return (value * jax.nn.sigmoid(gate)).astype(BF)
+
+    edge = glu(jnp.concatenate([nb[0, 7, ROWS - 16 :, :], nb[0, 0, :16, :]], axis=0))
+    gs[0] = edge[:16]
+    gs[1] = edge[16:]
     send(gs.at[0], gr.at[0], h_s.at[0], h_r.at[0], after)
     send(gs.at[1], gr.at[1], h_s.at[1], h_r.at[1], before)
-    gp[16 : 16 + TOK, :] = gated.astype(F32)
+    gp[16 : 16 + TOK, :] = glu(nb[0].reshape(TOK, D)).astype(F32)
+    pump()
     arrived(gr.at[0], h_s.at[0], h_r.at[0], before)
     arrived(gr.at[1], h_s.at[1], h_r.at[1], after)
     gp[0:16, :] = jnp.where(seq > 0, gr[0].astype(F32), 0.0)
@@ -328,11 +355,12 @@
         return carry
 
     lax.fori_loop(0, 4, depth, 0)
+    pump()
     need(2)
-    norm_two = branch(1, act, co, 1.0, (1, 2))
-    share(1, norm_two, 2)
+    branch(1, act, co, 1.0)
 
     need(3)
+    need(4)
 
     def ffn(j, carry):
         cols = pl.ds(pl.multiple_of(j * 256, 256), 256)
@@ -342,8 +370,9 @@
         return carry
 
     lax.fori_loop(0, 4, ffn, 0)
-    need(4)
-    out_ref[...] = branch(2, hid, fd, 0.5, (0, 0))
+    need(5)
+    need(6)
+    branch(2, hid, fd, 0.5)
     for d in pending:
         d.wait_send()
 
@@ -363,14 +392,15 @@
             v((2 * TOK, 128), F32), v((2 * TOK, 128), F32), v((2 * TOK, HD), F32),
             v((16, ROWS, HD), BF), v((8, ROWS, 256), BF),
             v((256, D), BF), v((D, 512), BF), v((256, D), BF), v((D, 1024), BF), v((1024, D), BF),
-            v((ROWS, D), BF), v((ROWS, D), F32), v((NY, ROWS, D), F32),
-            v((3, NY, ROWS, D), BF), v((3, NY, ROWS, D), BF), v((3, 3, ROWS, D), BF), v((3, 3, ROWS, D), BF),
+            v((ROWS, D), BF), v((ROWS, D), F32), v((CHUNKS, NY, 16, D), F32),
+            v((3, CHUNKS, NY, 16, D), BF), v((3, CHUNKS, NY, 16, D), BF), v((3, CHUNKS, 3, 16, D), BF), v((3, CHUNKS, 3, 16, D), BF),
             v((2, 8, ROWS, D), BF),
             v((TOK + 32, 256), F32), v((8, TOK + 24, 256), F32), v((2, 16, 256), BF), v((2, 16, 256), BF),
             v((8, ROWS, 256), BF), v((8, ROWS, 1024), BF), v((3, 1024), F32),
-            dma((11,)), dma((3,)), dma((3,)), dma((2, 2, 2)), dma((2, 2, 2)), dma((2, 2, 3)), dma((2, 2, 3)),
-            dma((5, 2, 4)), dma((5, 2, 4)), dma((5, 8)), dma((5, 8)), dma(()), dma(()),
-            dma((3,)), dma((3,)), dma((3, 3)), dma((3, 3)), dma((2, 3)), dma((2, 3)), dma((2, 4)), dma((2, 4)),
+            dma((13,)), dma((3,)), dma((3,)), dma((2, 2, 2)), dma((2, 2, 2)), dma((2, 2, 3)), dma((2, 2, 3)),
+            dma((7, 2, 4)), dma((7, 2, 4)), dma((7, 8)), dma((7, 8)), dma(()), dma(()),
+            dma((3, CHUNKS)), dma((3, CHUNKS)), dma((3, CHUNKS, 3)), dma((3, CHUNKS, 3)),
+            dma((2, CHUNKS, 3)), dma((2, CHUNKS, 3)), dma((2, CHUNKS, 4)), dma((2, CHUNKS, 4)),
             dma((2,)), dma((2,)),
         ],
         compiler_params=pltpu.CompilerParams(

time: 161 us -> 157 us (0.975)
  Pallas kernels: 159 us -> 155 us
    pallas_call x1, Pallas kernels: 159 us -> 155 us  [on_device(): pl.pallas_call(block_kernel, out_shape=jax.ShapeDtypeStruct((ROWS, D), F3...]
where the time goes in v2:
time: 157 us
  Pallas kernels  155 us (99%)
  local copies, waits for them, and re-layouts  1.77 us (1%)
    pallas_call x1, Pallas kernels, on_device(): pl.pallas_call(block_kernel, out_shape=jax.ShapeDtypeStruct((ROWS, D), F3...  155 us

profile of v2, /device:TPU:1, one launch (start us, length us, event | category | flops | bytes accessed | tf_op | source)
XLA Modules:
  0.0 157.0 jit_solution(15377953482478988317)
XLA Ops:
  0.0 155.3 %block.1 = f32[48,2048]{1,0:T(8,128)} custom-call(bf16[384,2048]{1,0:T(8,128)(2,1)} %res_hbm.1, bf16[384,256]{1,0:T(8,128)(2,1)} %q_hbm.1, bf16[384,256]{1,0:T(8,128)(2,1)} %k_hbm.1, bf16[384,256]{1,0:T(8,128)(2,1)} %v_hbm.1, bf16[256,128]{1,0:T(8,128)(2,1)} %wo_hbm.1, bf16[128,256]{1,0:T(8,128)(2,1)} %cval_hbm.1, bf16[128,256]{1,0:T(8,128)(2,1)} %cgate_hbm.1, ...), custom_call_target="tpu_custom_call" | custom-call | tf_op jit(solution)/shard_map/block/pallas_call | solution.py:385
  155.3 1.8 %copy.14 = f32[48,2048]{1,0:T(8,128)} copy(f32[48,2048]{1,0:T(8,128)} %block.1) | data formatting | bytes 786432

commit v3 on v2

--- a/solution.py
+++ b/solution.py
@@ -17,15 +17,17 @@
 D = 2048
 EPS = 1e-05
 TAPS = 31
-BQ = 256
 RIGHT, LEFT = 0, 1
 HOPS_A, HOPS_B = (4, 3), (3, 4)
-CHUNKS = ROWS // 16
+CHUNKS, GROUPS = ROWS // 16, 4
 RELAYS = [
-    (3, 0), (1, 1), (2, 1), (3, 1), (4, 0), (1, 2), (2, 2), (3, 2), (4, 1), (1, 3), (2, 3), (3, 3), (4, 2), (1, 4),
-    (2, 4), (5, 0), (3, 4), (4, 3), (6, 0), (5, 1), (4, 4), (6, 1), (5, 2), (6, 2), (5, 3), (6, 3), (5, 4), (6, 4),
+    (1, 0), (3, 0), (1, 1), (2, 0), (4, 0), (2, 1), (1, 2), (3, 1), (1, 3), (4, 1), (2, 2), (5, 0),
+    (1, 4), (2, 3), (4, 2), (6, 0), (2, 4), (3, 2), (5, 1), (3, 3), (4, 3), (6, 1), (5, 2), (3, 4),
+    (6, 2), (4, 4), (6, 3), (5, 3), (6, 4), (5, 4),
 ]
-PUMPS = [3] + [1, 1, 1, 1, 1, 1, 1, 1] + [1, 1] + [1, 1, 1, 1, 1, 1, 1, 1] + [0, 0, 0, 0]
+PUMPS = [
+    0, 0, 1, 1, 0, 3, 0, 3, 0, 4, 1, 0, 3, 2, 1, 0, 0, 4, 1, 2, 0, 2, 0, 2,
+]
 
 
 def layer_norm(x):
@@ -38,10 +40,10 @@
 def block_kernel(
     res_hbm, q_hbm, k_hbm, v_hbm, wo_hbm, cval_hbm, cgate_hbm, dk_ref, co_hbm, fi_hbm, fd_hbm, mask_ref,
     out_ref,
-    qb, kb, vb, m_s, l_s, acc, ob, ho, wo, cv, co, fi, fd, res, stream, ps, xs, xr, rs, rr, nb,
+    qb, kb, vb, m_s, l_s, acc, ob, ho, wo, cv, co, fi, fd, res, stream, ps, xs, xr, rs, rr, ps3, xs3, xr3, rs3, rr3, nb,
     gp, sh, gs, gr, act, hid, mrow,
     loc, qx_s, qx_r, kv1_s, kv1_r, kv_s, kv_r, wz_s, wz_r, wx_s, wx_r, o_s, o_r,
-    pc_s, pc_r, rx_s, rx_r, ag_s, ag_r, agc_s, agc_r, h_s, h_r,
+    pc_s, pc_r, rx_s, rx_r, ag_s, ag_r, agc_s, agc_r, pc3_s, pc3_r, rx3_s, rx3_r, h_s, h_r,
 ):
     seq, mp, dp = lax.axis_index("seq"), lax.axis_index("mp"), lax.axis_index("dp")
     lo, z = lax.div(seq, NZ), lax.rem(seq, NZ)
@@ -176,11 +178,13 @@
                 send(ref, ref, wz_s.at[p, w, s], wz_r.at[p, w, s], to)
             x_send(p, 7 if s == 4 else 2 * s - 1 + w, shard)
 
-    def weights_done(p):
-        for k in range(8):
-            shard = z if k == 0 else z + 4 if k == 7 else z - (k + 1) // 2 if k % 2 else z + k // 2
+    def shard_of(k):
+        return zmod(z if k == 0 else z - (k + 1) // 2 if k % 2 else z + k // 2)
+
+    def weights_done(p, ks=range(8)):
+        for k in ks:
             frm = xl_dev if x_way(p, k) == RIGHT else xr_dev
-            arrived(slots[p]((1 - lo) * NZ + zmod(shard)), wx_s.at[p, k], wx_r.at[p, k], frm)
+            arrived(slots[p]((1 - lo) * NZ + shard_of(k)), wx_s.at[p, k], wx_r.at[p, k], frm)
 
     todo = list(RELAYS)
     counts = list(PUMPS)
@@ -200,9 +204,9 @@
 
     scale2 = math.log2(math.e) / math.sqrt(HD)
 
-    def attend(slot, first=False):
+    def attend(slot, first=False, base=0, steps=3, size=256):
         def body(i, carry):
-            rows = pl.ds(pl.multiple_of(i * BQ, BQ), BQ)
+            rows = pl.ds(pl.multiple_of(base + i * size, 64), size)
             s = lax.dot_general(
                 qb[rows, :], kb[slot], (((1,), (1,)), ((), ())), preferred_element_type=F32
             )
@@ -219,12 +223,12 @@
                 shrink = jnp.exp2((old - top) * scale2)
                 part = part + l_s[rows, :] * shrink
                 out = out + acc[rows, :] * shrink
-            m_s[rows, :] = jnp.broadcast_to(top, (BQ, 128))
+            m_s[rows, :] = jnp.broadcast_to(top, (size, 128))
             l_s[rows, :] = part
             acc[rows, :] = out
             return carry
 
-        lax.fori_loop(0, 2 * TOK // BQ, body, 0)
+        lax.fori_loop(0, steps, body, 0)
 
     for d in own[0]:
         d.wait()
@@ -241,22 +245,25 @@
     lv.wait()
     arrived(qb.at[far_rows, :], qx_s.at[2], qx_r.at[2], pair)
     attend(z, first=True)
+    def finish(rows, blocks):
+        o = acc[rows, :] / jnp.sum(l_s[rows, :], axis=1, keepdims=True)
+        ob[blocks] = o.astype(BF).reshape(8, ROWS, HD)
+
+    far_blocks, own_blocks = pl.ds((1 - lo) * 8, 8), pl.ds(lo * 8, 8)
     for s in (1, 2, 3, 4):
         kv_relay(0, s)
         if s > 1:
             attend(zmod(z + s - 1))
         kv_relay(1, s)
         relay(0, s)
-        if s in (2, 3):
-            begin(s - 1)
-        attend(zmod(z - s))
-    def finish(rows, blocks):
-        o = acc[rows, :] / jnp.sum(l_s[rows, :], axis=1, keepdims=True)
-        ob[blocks] = o.astype(BF).reshape(8, ROWS, HD)
-
-    far_blocks, own_blocks = pl.ds((1 - lo) * 8, 8), pl.ds(lo * 8, 8)
+        pump()
+        if s < 4:
+            attend(zmod(z - s))
+    attend(zmod(z + 4), base=(1 - lo) * TOK, steps=2, size=192)
     finish(far_rows, far_blocks)
     send(ob.at[far_blocks], ho.at[:, :, own_cols], o_s, o_r, pair)
+    pump()
+    attend(zmod(z + 4), base=lo * TOK, steps=2, size=192)
     finish(own_rows, own_blocks)
     lo_copy = local(ob.at[own_blocks], ho.at[:, :, own_cols], 12)
     for i in range(3):
@@ -268,7 +275,7 @@
     pump()
     arrived(ho.at[:, :, far_cols], o_s, o_r, pair)
 
-    def branch(n, left, weight, factor):
+    def branch(n, left, weight):
         for mine in (False, True):
             side = c if mine else 1 - c
             lhs = jnp.concatenate([left[2 * b + side] for b in range(NY)], axis=0)
@@ -298,18 +305,13 @@
             for d in (1, 3, 2):
                 arrived(rr.at[n, r, d - 1], rx_s.at[n, r, d - 1], rx_r.at[n, r, d - 1], ys[3 - d])
                 total = total + rr[n, r, d - 1].astype(F32)
-            new = stream[rows, :] + factor * total
-            if n == 2:
-                out_ref[rows, :] = layer_norm(new)
-                continue
+            new = stream[rows, :] + total
             stream[rows, :] = new
             mine = nb.at[n, mp, rows]
             nb[n, mp, rows] = layer_norm(new).astype(BF)
             for d in (2, 1, 3):
                 send(mine, mine, ag_s.at[n, r, d - 1], ag_r.at[n, r, d - 1], ys[d - 1])
             send(mine, mine, agc_s.at[n, r, 0], agc_r.at[n, r, 0], core)
-        if n == 2:
-            return
         for r in range(CHUNKS):
             pump()
             rows = slice(r * 16, (r + 1) * 16)
@@ -324,7 +326,7 @@
                 arrived(nb.at[n, 2 * ymod(y - d) + 1 - c, rows], agc_s.at[n, r, d], agc_r.at[n, r, d], core)
 
     need(0)
-    branch(0, ho, wo, 1.0)
+    branch(0, ho, wo)
 
     need(1)
 
@@ -357,7 +359,7 @@
     lax.fori_loop(0, 4, depth, 0)
     pump()
     need(2)
-    branch(1, act, co, 1.0)
+    branch(1, act, co)
 
     need(3)
     need(4)
@@ -370,9 +372,40 @@
         return carry
 
     lax.fori_loop(0, 4, ffn, 0)
-    need(5)
-    need(6)
-    branch(2, hid, fd, 0.5)
+    def columns(g):
+        return [
+            pl.ds(pl.multiple_of((side * NZ + shard_of(k)) * 128, 128), 128)
+            for side in (lo, 1 - lo) for k in (2 * g, 2 * g + 1)
+        ]
+
+    for g in range(GROUPS):
+        while (5, g + 1) in todo or (6, g + 1) in todo:
+            pump(1)
+        for p in (5, 6):
+            weights_done(p, (2 * g, 2 * g + 1))
+        rhs = jnp.concatenate([fd[:, cols] for cols in columns(g)], axis=1)
+        for mine in (False, True):
+            side = c if mine else 1 - c
+            lhs = jnp.concatenate([hid[2 * b + side] for b in range(NY)], axis=0)
+            prod = jnp.dot(lhs, rhs, preferred_element_type=F32).reshape(NY, ROWS, 512)
+            if mine:
+                ps3[g] = prod
+            else:
+                xs3[g] = prod.astype(BF)
+                send(xs3.at[g], xr3.at[g], pc3_s.at[g], pc3_r.at[g], core)
+        arrived(xr3.at[g], pc3_s.at[g], pc3_r.at[g], core)
+        for d in (2, 1, 3):
+            b = ymod(y + d)
+            rs3[g, d - 1] = (ps3[g, b] + xr3[g, b].astype(F32)).astype(BF)
+            send(rs3.at[g, d - 1], rr3.at[g, d - 1], rx3_s.at[g, d - 1], rx3_r.at[g, d - 1], ys[d - 1])
+    for g in range(GROUPS):
+        total = ps3[g, y] + xr3[g, y].astype(F32)
+        for d in (1, 3, 2):
+            arrived(rr3.at[g, d - 1], rx3_s.at[g, d - 1], rx3_r.at[g, d - 1], ys[3 - d])
+            total = total + rr3[g, d - 1].astype(F32)
+        for i, cols in enumerate(columns(g)):
+            stream[:, cols] += 0.5 * total[:, i * 128 : (i + 1) * 128]
+    out_ref[...] = layer_norm(stream[...])
     for d in pending:
         d.wait_send()
 
@@ -393,14 +426,18 @@
             v((16, ROWS, HD), BF), v((8, ROWS, 256), BF),
             v((256, D), BF), v((D, 512), BF), v((256, D), BF), v((D, 1024), BF), v((1024, D), BF),
             v((ROWS, D), BF), v((ROWS, D), F32), v((CHUNKS, NY, 16, D), F32),
-            v((3, CHUNKS, NY, 16, D), BF), v((3, CHUNKS, NY, 16, D), BF), v((3, CHUNKS, 3, 16, D), BF), v((3, CHUNKS, 3, 16, D), BF),
+            v((2, CHUNKS, NY, 16, D), BF), v((2, CHUNKS, NY, 16, D), BF),
+            v((2, CHUNKS, 3, 16, D), BF), v((2, CHUNKS, 3, 16, D), BF),
+            v((GROUPS, NY, ROWS, 512), F32), v((GROUPS, NY, ROWS, 512), BF), v((GROUPS, NY, ROWS, 512), BF),
+            v((GROUPS, 3, ROWS, 512), BF), v((GROUPS, 3, ROWS, 512), BF),
             v((2, 8, ROWS, D), BF),
             v((TOK + 32, 256), F32), v((8, TOK + 24, 256), F32), v((2, 16, 256), BF), v((2, 16, 256), BF),
             v((8, ROWS, 256), BF), v((8, ROWS, 1024), BF), v((3, 1024), F32),
             dma((13,)), dma((3,)), dma((3,)), dma((2, 2, 2)), dma((2, 2, 2)), dma((2, 2, 3)), dma((2, 2, 3)),
             dma((7, 2, 4)), dma((7, 2, 4)), dma((7, 8)), dma((7, 8)), dma(()), dma(()),
-            dma((3, CHUNKS)), dma((3, CHUNKS)), dma((3, CHUNKS, 3)), dma((3, CHUNKS, 3)),
+            dma((2, CHUNKS)), dma((2, CHUNKS)), dma((2, CHUNKS, 3)), dma((2, CHUNKS, 3)),
             dma((2, CHUNKS, 3)), dma((2, CHUNKS, 3)), dma((2, CHUNKS, 4)), dma((2, CHUNKS, 4)),
+            dma((GROUPS,)), dma((GROUPS,)), dma((GROUPS, 3)), dma((GROUPS, 3)),
             dma((2,)), dma((2,)),
         ],
         compiler_params=pltpu.CompilerParams(

time: 157 us -> 133 us (0.85)
  Pallas kernels: 155 us -> 131 us
    pallas_call x1, Pallas kernels: 155 us -> 131 us  [on_device(): pl.pallas_call(block_kernel, out_shape=jax.ShapeDtypeStruct((ROWS, D), F3...]
where the time goes in v3:
time: 133 us
  Pallas kernels  131 us (98%)
  local copies, waits for them, and re-layouts  1.77 us (1%)
    pallas_call x1, Pallas kernels, on_device(): pl.pallas_call(block_kernel, out_shape=jax.ShapeDtypeStruct((ROWS, D), F3...  131 us

profile of v3, /device:TPU:1, one launch (start us, length us, event | category | flops | bytes accessed | tf_op | source)
XLA Modules:
  0.0 132.9 jit_solution(14438931295100859941)
XLA Ops:
  0.0 131.1 %block.1 = f32[48,2048]{1,0:T(8,128)} custom-call(bf16[384,2048]{1,0:T(8,128)(2,1)} %res_hbm.1, bf16[384,256]{1,0:T(8,128)(2,1)} %q_hbm.1, bf16[384,256]{1,0:T(8,128)(2,1)} %k_hbm.1, bf16[384,256]{1,0:T(8,128)(2,1)} %v_hbm.1, bf16[256,128]{1,0:T(8,128)(2,1)} %wo_hbm.1, bf16[128,256]{1,0:T(8,128)(2,1)} %cval_hbm.1, bf16[128,256]{1,0:T(8,128)(2,1)} %cgate_hbm.1, ...), custom_call_target="tpu_custom_call" | custom-call | tf_op jit(solution)/shard_map/block/pallas_call | solution.py:418
  131.2 1.8 %copy.14 = f32[48,2048]{1,0:T(8,128)} copy(f32[48,2048]{1,0:T(8,128)} %block.1) | data formatting | bytes 786432

commit v4 on v3

--- a/solution.py
+++ b/solution.py
@@ -21,12 +21,13 @@
 HOPS_A, HOPS_B = (4, 3), (3, 4)
 CHUNKS, GROUPS = ROWS // 16, 4
 RELAYS = [
-    (1, 0), (3, 0), (1, 1), (2, 0), (4, 0), (2, 1), (1, 2), (3, 1), (1, 3), (4, 1), (2, 2), (5, 0),
-    (1, 4), (2, 3), (4, 2), (6, 0), (2, 4), (3, 2), (5, 1), (3, 3), (4, 3), (6, 1), (5, 2), (3, 4),
-    (6, 2), (4, 4), (6, 3), (5, 3), (6, 4), (5, 4),
+    (1, 0), (2, 0), (4, 0), (1, 1), (2, 1), (3, 0), (1, 2), (2, 2), (4, 1), (1, 3), (5, 0), (2, 3),
+    (3, 1), (1, 4), (2, 4), (6, 0), (5, 1), (3, 2), (6, 1), (4, 2), (3, 3), (6, 2), (4, 3), (5, 2),
+    (3, 4), (4, 4), (6, 3), (5, 3), (6, 4), (5, 4),
 ]
 PUMPS = [
-    0, 0, 1, 1, 0, 3, 0, 3, 0, 4, 1, 0, 3, 2, 1, 0, 0, 4, 1, 2, 0, 2, 0, 2,
+    1, 0, 0, 0, 0, 0, 3, 0, 0, 2, 0, 1, 4, 2, 0, 0, 0, 1, 0, 3, 1, 0, 0, 2,
+    0, 0, 4, 1, 0, 0, 2, 0, 1, 0, 2, 0, 0,
 ]
 
 
@@ -65,7 +66,8 @@
     xl_dev = dev(other_seq, mp, lax.rem(dp + 1 - lo, 2))
     pair = dev(other_seq, mp, dp)
     core = dev(seq, 2 * y + 1 - c, dp)
-    ys = [dev(seq, 2 * ymod(y + d) + c, dp) for d in (1, 2, 3)]
+    yr, yl = dev(seq, 2 * ymod(y + 1) + c, dp), dev(seq, 2 * ymod(y - 1) + c, dp)
+    yo = dev(seq, 2 * ymod(y + 2) + c, dp)
     after = dev(lax.rem(seq + 1, 2 * NZ), mp, dp)
     before = dev(lax.rem(seq + 2 * NZ - 1, 2 * NZ), mp, dp)
 
@@ -118,7 +120,7 @@
     lres = local(res_hbm.at[pl.ds(pl.multiple_of(mp * ROWS, ROWS), ROWS), :], res, 11)
 
     bar = pltpu.get_barrier_semaphore()
-    peers = [zr, zl, xr_dev, xl_dev, core, *ys, after, before]
+    peers = [zr, zl, xr_dev, xl_dev, core, yr, yl, yo, after, before]
     for p in peers:
         pl.semaphore_signal(bar, inc=1, device_id=p, device_id_type=MESH)
     pl.semaphore_wait(bar, len(peers))
@@ -204,8 +206,8 @@
 
     scale2 = math.log2(math.e) / math.sqrt(HD)
 
-    def attend(slot, first=False, base=0, steps=3, size=256):
-        def body(i, carry):
+    def attend(slot, first=False, base=0, steps=2, size=384):
+        for i in range(steps):
             rows = pl.ds(pl.multiple_of(base + i * size, 64), size)
             s = lax.dot_general(
                 qb[rows, :], kb[slot], (((1,), (1,)), ((), ())), preferred_element_type=F32
@@ -226,9 +228,6 @@
             m_s[rows, :] = jnp.broadcast_to(top, (size, 128))
             l_s[rows, :] = part
             acc[rows, :] = out
-            return carry
-
-        lax.fori_loop(0, steps, body, 0)
 
     for d in own[0]:
         d.wait()
@@ -240,6 +239,7 @@
             for d in own[p]:
                 d.wait()
         x_send(p, 0, z)
+    pump()
     lq.wait()
     lk.wait()
     lv.wait()
@@ -252,6 +252,7 @@
     far_blocks, own_blocks = pl.ds((1 - lo) * 8, 8), pl.ds(lo * 8, 8)
     for s in (1, 2, 3, 4):
         kv_relay(0, s)
+        pump()
         if s > 1:
             attend(zmod(z + s - 1))
         kv_relay(1, s)
@@ -275,6 +276,47 @@
     pump()
     arrived(ho.at[:, :, far_cols], o_s, o_r, pair)
 
+    class Scatter:
+        def __init__(self, part, out, got, ssem, rsem):
+            self.part, self.out, self.got, self.ssem, self.rsem = part, out, got, ssem, rsem
+
+        def put(self, i, value):
+            self.out[i] = value.astype(BF)
+            send(self.out.at[i], self.got.at[i], self.ssem.at[i], self.rsem.at[i], yl if i % 2 else yr)
+
+        def take(self, i):
+            arrived(self.got.at[i], self.ssem.at[i], self.rsem.at[i], yr if i % 2 else yl)
+            return self.got[i].astype(F32)
+
+        def first(self):
+            right, left, far = ymod(y + 1), ymod(y - 1), ymod(y + 2)
+            self.put(0, self.part(far, 0))
+            self.put(1, self.part(far, 1))
+            self.put(2, self.part(right, 1))
+            self.put(3, self.part(left, 0))
+
+        def direct(self):
+            right, left, far = ymod(y + 1), ymod(y - 1), ymod(y + 2)
+            for i, (b, to) in enumerate(((far, yo), (far, yo), (right, yr), (left, yl), (right, yr), (left, yl))):
+                self.out[i] = self.part(b, (0, 1, 1, 0, 0, 1)[i]).astype(BF)
+                send(self.out.at[i], self.got.at[i], self.ssem.at[i], self.rsem.at[i], to)
+
+        def direct_total(self):
+            halves = [self.part(y, 0), self.part(y, 1)]
+            for i, frm in ((3, yr), (4, yl), (2, yl), (5, yr), (0, yo), (1, yo)):
+                arrived(self.got.at[i], self.ssem.at[i], self.rsem.at[i], frm)
+                halves[(0, 1, 1, 0, 0, 1)[i]] += self.got[i].astype(F32)
+            return jnp.concatenate(halves, axis=1)
+
+        def second(self):
+            self.put(4, self.part(ymod(y + 1), 0) + self.take(0))
+            self.put(5, self.part(ymod(y - 1), 1) + self.take(1))
+
+        def total(self):
+            low = self.part(y, 0) + self.take(3) + self.take(4)
+            high = self.part(y, 1) + self.take(2) + self.take(5)
+            return jnp.concatenate([low, high], axis=1)
+
     def branch(n, left, weight):
         for mine in (False, True):
             side = c if mine else 1 - c
@@ -292,34 +334,60 @@
                 for r in range(CHUNKS):
                     send(xs.at[n, r], xr.at[n, r], pc_s.at[n, r], pc_r.at[n, r], core)
                 pump()
+        half = D // 2
+
+        def part_of(r):
+            def part(b, h):
+                cols = slice(h * half, (h + 1) * half)
+                return ps[r, b, :, cols] + xr[n, r, b, :, cols].astype(F32)
+
+            return part
+
+        chunks = [
+            Scatter(part_of(r), rs.at[n, r], rr.at[n, r], rx_s.at[n, r], rx_r.at[n, r]) for r in range(CHUNKS)
+        ]
         for r in range(CHUNKS):
             arrived(xr.at[n, r], pc_s.at[n, r], pc_r.at[n, r], core)
-            for d in (2, 1, 3):
-                b = ymod(y + d)
-                rs[n, r, d - 1] = (ps[r, b] + xr[n, r, b].astype(F32)).astype(BF)
-                send(rs.at[n, r, d - 1], rr.at[n, r, d - 1], rx_s.at[n, r, d - 1], rx_r.at[n, r, d - 1], ys[d - 1])
+            if r:
+                chunks[r].first()
+            else:
+                chunks[r].direct()
+        for r in range(1, CHUNKS):
+            pump()
+            chunks[r].second()
         for r in range(CHUNKS):
             pump()
             rows = slice(r * 16, (r + 1) * 16)
-            total = ps[r, y] + xr[n, r, y].astype(F32)
-            for d in (1, 3, 2):
-                arrived(rr.at[n, r, d - 1], rx_s.at[n, r, d - 1], rx_r.at[n, r, d - 1], ys[3 - d])
-                total = total + rr[n, r, d - 1].astype(F32)
-            new = stream[rows, :] + total
+            new = stream[rows, :] + (chunks[r].total() if r else chunks[r].direct_total())
             stream[rows, :] = new
+            nb[n, mp, rows] = layer_norm(new).astype(BF)
             mine = nb.at[n, mp, rows]
-            nb[n, mp, rows] = layer_norm(new).astype(BF)
-            for d in (2, 1, 3):
-                send(mine, mine, ag_s.at[n, r, d - 1], ag_r.at[n, r, d - 1], ys[d - 1])
+            send(mine, mine, ag_s.at[n, r, 0], ag_r.at[n, r, 0], yr)
+            send(mine, mine, ag_s.at[n, r, 1], ag_r.at[n, r, 1], yl)
+            if r == CHUNKS - 1:
+                send(mine, mine, ag_s.at[n, r, 2], ag_r.at[n, r, 2], yo)
             send(mine, mine, agc_s.at[n, r, 0], agc_r.at[n, r, 0], core)
         for r in range(CHUNKS):
             pump()
             rows = slice(r * 16, (r + 1) * 16)
-            for d in (1, 3, 2):
-                got = nb.at[n, 2 * ymod(y - d) + c, rows]
-                arrived(got, ag_s.at[n, r, d - 1], ag_r.at[n, r, d - 1], ys[3 - d])
+            for i, (d, frm, to) in enumerate(((1, yl, yr), (3, yr, yl))):
+                b = 2 * ymod(y - d) + c
+                got, part = nb.at[n, b, rows], nb.at[n, b, rows, i * half : (i + 1) * half]
+                arrived(got, ag_s.at[n, r, i], ag_r.at[n, r, i], frm)
+                if r < CHUNKS - 1:
+                    send(part, part, ag_s.at[n, r, 2 + i], ag_r.at[n, r, 2 + i], to)
                 send(got, got, agc_s.at[n, r, d], agc_r.at[n, r, d], core)
-        pump()
+        for r in range(CHUNKS):
+            pump()
+            rows = slice(r * 16, (r + 1) * 16)
+            b = 2 * ymod(y + 2) + c
+            if r < CHUNKS - 1:
+                for i, frm in enumerate((yl, yr)):
+                    part = nb.at[n, b, rows, i * half : (i + 1) * half]
+                    arrived(part, ag_s.at[n, r, 2 + i], ag_r.at[n, r, 2 + i], frm)
+            else:
+                arrived(nb.at[n, b, rows], ag_s.at[n, r, 2], ag_r.at[n, r, 2], yo)
+            send(nb.at[n, b, rows], nb.at[n, b, rows], agc_s.at[n, r, 2], agc_r.at[n, r, 2], core)
         for r in range(CHUNKS):
             rows = slice(r * 16, (r + 1) * 16)
             for d in (0, 1, 3, 2):
@@ -377,6 +445,14 @@
             pl.ds(pl.multiple_of((side * NZ + shard_of(k)) * 128, 128), 128)
             for side in (lo, 1 - lo) for k in (2 * g, 2 * g + 1)
         ]
+
+    def part_of(g):
+        return lambda b, h: ps3[g, b, :, h * 256 : (h + 1) * 256] + xr3[g, b, :, h * 256 : (h + 1) * 256].astype(F32)
+
+    groups = [Scatter(part_of(g), rs3.at[g], rr3.at[g], rx3_s.at[g], rx3_r.at[g]) for g in range(GROUPS)]
+    def open_group(g):
+        arrived(xr3.at[g], pc3_s.at[g], pc3_r.at[g], core)
+        groups[g].first()
 
     for g in range(GROUPS):
         while (5, g + 1) in todo or (6, g + 1) in todo:
@@ -393,16 +469,15 @@
             else:
                 xs3[g] = prod.astype(BF)
                 send(xs3.at[g], xr3.at[g], pc3_s.at[g], pc3_r.at[g], core)
-        arrived(xr3.at[g], pc3_s.at[g], pc3_r.at[g], core)
-        for d in (2, 1, 3):
-            b = ymod(y + d)
-            rs3[g, d - 1] = (ps3[g, b] + xr3[g, b].astype(F32)).astype(BF)
-            send(rs3.at[g, d - 1], rr3.at[g, d - 1], rx3_s.at[g, d - 1], rx3_r.at[g, d - 1], ys[d - 1])
+        if g:
+            open_group(g - 1)
+        if g > 1:
+            groups[g - 2].second()
+    arrived(xr3.at[GROUPS - 1], pc3_s.at[GROUPS - 1], pc3_r.at[GROUPS - 1], core)
+    groups[GROUPS - 1].direct()
+    groups[GROUPS - 2].second()
     for g in range(GROUPS):
-        total = ps3[g, y] + xr3[g, y].astype(F32)
-        for d in (1, 3, 2):
-            arrived(rr3.at[g, d - 1], rx3_s.at[g, d - 1], rx3_r.at[g, d - 1], ys[3 - d])
-            total = total + rr3[g, d - 1].astype(F32)
+        total = groups[g].total() if g < GROUPS - 1 else groups[g].direct_total()
         for i, cols in enumerate(columns(g)):
             stream[:, cols] += 0.5 * total[:, i * 128 : (i + 1) * 128]
     out_ref[...] = layer_norm(stream[...])
@@ -427,17 +502,17 @@
             v((256, D), BF), v((D, 512), BF), v((256, D), BF), v((D, 1024), BF), v((1024, D), BF),
             v((ROWS, D), BF), v((ROWS, D), F32), v((CHUNKS, NY, 16, D), F32),
             v((2, CHUNKS, NY, 16, D), BF), v((2, CHUNKS, NY, 16, D), BF),
-            v((2, CHUNKS, 3, 16, D), BF), v((2, CHUNKS, 3, 16, D), BF),
+            v((2, CHUNKS, 6, 16, D // 2), BF), v((2, CHUNKS, 6, 16, D // 2), BF),
             v((GROUPS, NY, ROWS, 512), F32), v((GROUPS, NY, ROWS, 512), BF), v((GROUPS, NY, ROWS, 512), BF),
-            v((GROUPS, 3, ROWS, 512), BF), v((GROUPS, 3, ROWS, 512), BF),
+            v((GROUPS, 6, ROWS, 256), BF), v((GROUPS, 6, ROWS, 256), BF),
             v((2, 8, ROWS, D), BF),
             v((TOK + 32, 256), F32), v((8, TOK + 24, 256), F32), v((2, 16, 256), BF), v((2, 16, 256), BF),
             v((8, ROWS, 256), BF), v((8, ROWS, 1024), BF), v((3, 1024), F32),
             dma((13,)), dma((3,)), dma((3,)), dma((2, 2, 2)), dma((2, 2, 2)), dma((2, 2, 3)), dma((2, 2, 3)),
             dma((7, 2, 4)), dma((7, 2, 4)), dma((7, 8)), dma((7, 8)), dma(()), dma(()),
-            dma((2, CHUNKS)), dma((2, CHUNKS)), dma((2, CHUNKS, 3)), dma((2, CHUNKS, 3)),
-            dma((2, CHUNKS, 3)), dma((2, CHUNKS, 3)), dma((2, CHUNKS, 4)), dma((2, CHUNKS, 4)),
-            dma((GROUPS,)), dma((GROUPS,)), dma((GROUPS, 3)), dma((GROUPS, 3)),
+            dma((2, CHUNKS)), dma((2, CHUNKS)), dma((2, CHUNKS, 6)), dma((2, CHUNKS, 6)),
+            dma((2, CHUNKS, 4)), dma((2, CHUNKS, 4)), dma((2, CHUNKS, 4)), dma((2, CHUNKS, 4)),
+            dma((GROUPS,)), dma((GROUPS,)), dma((GROUPS, 6)), dma((GROUPS, 6)),
             dma((2,)), dma((2,)),
         ],
         compiler_params=pltpu.CompilerParams(

time: 133 us -> 130 us (0.977)
  Pallas kernels: 131 us -> 128 us
    pallas_call x1, Pallas kernels: 131 us -> 128 us  [on_device(): pl.pallas_call(block_kernel, out_shape=jax.ShapeDtypeStruct((ROWS, D), F3...]
where the time goes in v4:
time: 130 us
  Pallas kernels  128 us (98%)
  local copies, waits for them, and re-layouts  1.77 us (1%)
    pallas_call x1, Pallas kernels, on_device(): pl.pallas_call(block_kernel, out_shape=jax.ShapeDtypeStruct((ROWS, D), F3...  128 us

profile of v4, /device:TPU:1, one launch (start us, length us, event | category | flops | bytes accessed | tf_op | source)
XLA Modules:
  0.0 129.9 jit_solution(12987059222916171758)
XLA Ops:
  0.0 128.1 %block.1 = f32[48,2048]{1,0:T(8,128)} custom-call(bf16[384,2048]{1,0:T(8,128)(2,1)} %res_hbm.1, bf16[384,256]{1,0:T(8,128)(2,1)} %q_hbm.1, bf16[384,256]{1,0:T(8,128)(2,1)} %k_hbm.1, bf16[384,256]{1,0:T(8,128)(2,1)} %v_hbm.1, bf16[256,128]{1,0:T(8,128)(2,1)} %wo_hbm.1, bf16[128,256]{1,0:T(8,128)(2,1)} %cval_hbm.1, bf16[128,256]{1,0:T(8,128)(2,1)} %cgate_hbm.1, ...), custom_call_target="tpu_custom_call" | custom-call | tf_op jit(solution)/shard_map/block/pallas_call | solution.py:493
  128.1 1.8 %copy.14 = f32[48,2048]{1,0:T(8,128)} copy(f32[48,2048]{1,0:T(8,128)} %block.1) | data formatting | bytes 786432

commit v5 on v4

--- a/solution.py
+++ b/solution.py
@@ -471,11 +471,10 @@
                 send(xs3.at[g], xr3.at[g], pc3_s.at[g], pc3_r.at[g], core)
         if g:
             open_group(g - 1)
-        if g > 1:
-            groups[g - 2].second()
     arrived(xr3.at[GROUPS - 1], pc3_s.at[GROUPS - 1], pc3_r.at[GROUPS - 1], core)
     groups[GROUPS - 1].direct()
-    groups[GROUPS - 2].second()
+    for g in range(GROUPS - 1):
+        groups[g].second()
     for g in range(GROUPS):
         total = groups[g].total() if g < GROUPS - 1 else groups[g].direct_total()
         for i, cols in enumerate(columns(g)):

time: 130 us -> 129 us (level)
  no operation moved by 1% of the time
where the time goes in v5:
time: 129 us
  Pallas kernels  127 us (98%)
  local copies, waits for them, and re-layouts  1.77 us (1%)
    pallas_call x1, Pallas kernels, on_device(): pl.pallas_call(block_kernel, out_shape=jax.ShapeDtypeStruct((ROWS, D), F3...  127 us

profile of v5, /device:TPU:1, one launch (start us, length us, event | category | flops | bytes accessed | tf_op | source)
XLA Modules:
  0.0 129.1 jit_solution(11482275159987255363)
XLA Ops:
  0.0 127.3 %block.1 = f32[48,2048]{1,0:T(8,128)} custom-call(bf16[384,2048]{1,0:T(8,128)(2,1)} %res_hbm.1, bf16[384,256]{1,0:T(8,128)(2,1)} %q_hbm.1, bf16[384,256]{1,0:T(8,128)(2,1)} %k_hbm.1, bf16[384,256]{1,0:T(8,128)(2,1)} %v_hbm.1, bf16[256,128]{1,0:T(8,128)(2,1)} %wo_hbm.1, bf16[128,256]{1,0:T(8,128)(2,1)} %cval_hbm.1, bf16[128,256]{1,0:T(8,128)(2,1)} %cgate_hbm.1, ...), custom_call_target="tpu_custom_call" | custom-call | tf_op jit(solution)/shard_map/block/pallas_call | solution.py:492
  127.3 1.8 %copy.14 = f32[48,2048]{1,0:T(8,128)} copy(f32[48,2048]{1,0:T(8,128)} %block.1) | data formatting | bytes 786432
